TPU v7x, 256 devices: a whole 4x4x8 slice. The times are simulated.
256 devices in a mesh: section: 4 (over y), seq: 64 (over z, x, core).
Axes of the slice: x: 4, y: 4, z: 8, core: 2. Of those that a mesh axis runs over, the one named last changes fastest.
Arguments:
- span_inputs: bfloat16 [4, 2048, 3, 8192], P('section', 'seq'), may hold values from -28 to 28
- out_grad: bfloat16 [4, 2048, 8192], P('section', 'seq'), may hold values from -48 to 48
- past_cache: bfloat16 [4, 3072, 2, 64, 128], P('section', None, None, 'seq'), may hold values from -5 to 5
- past_accum: float32 [4, 3072, 2, 64, 128], P('section', None, None, 'seq'), may hold values from -0.6 to 0.6
- offsets: int32 [4], P('section'), may hold values from 0 to 3072, as said below
- lengths: int32 [4], P('section'), may hold values from 1024 to 2048, as said below
Outputs:
- next_grads: bfloat16 [4, 2048, 3, 8192], P('section', 'seq')
- new_accum: float32 [4, 3072, 2, 64, 128], P('section', None, None, 'seq')
Inputs may be any that keep to these rules, and one draw needn't show every extreme that they name: The first offsets[s] rows of past_cache[s] and past_accum[s] belong to the sequence; one section's offset is 3072. Rows of a span from lengths[s] on are padding; one section's length is 2048.
All inputs are finite; a program needn't handle non-finite values.
Results may differ from a plain program's by a relative error of at most 0.0068.
Values may be sent and summed in bfloat16 or wider, within the bound.
No kernel may reach another device: no remote copies, remote signals or barrier semaphores. Data moves between devices by JAX's collectives and lax.ppermute only.
A program may use at most 128 MiB of HBM per device.

v0:
```python
import math

import jax
import jax.numpy as jnp
from jax import lax
from jax.sharding import PartitionSpec as P

HEADS = 64
DH = 128


def from_behind(block, axis, distance):
    devices = range(lax.axis_size(axis))
    route = [((i - distance) % len(devices), i) for i in devices]
    return lax.ppermute(block, axis, route)


def per_device(span_inputs, out_grad, past_cache, past_accum, offsets, lengths):
    scale_factor = 1.0 / math.sqrt(DH)
    tok_rows = span_inputs.shape[1]
    local_rows = span_inputs[0].reshape(tok_rows, 3, HEADS, DH)
    upstream = out_grad[0].reshape(tok_rows, 1, HEADS, DH)
    offset = offsets[0]
    length = lengths[0]
    cached = past_cache[0]
    past_len = cached.shape[0]
    head_inputs, head_dout = (
        lax.all_to_all(local_rows, "seq", split_axis=2, concat_axis=0, tiled=True),
        lax.all_to_all(upstream, "seq", split_axis=2, concat_axis=0, tiled=True),
    )
    span_len = head_inputs.shape[0]
    local_heads = head_inputs.shape[2]
    block_rows = min(512, span_len)
    block_count = span_len // block_rows
    all_keys = jnp.concatenate([cached[:, 0], head_inputs[:, 1]], axis=0)
    all_values = jnp.concatenate([cached[:, 1], head_inputs[:, 2]], axis=0)
    key_count = all_keys.shape[0]
    queries = head_inputs[:, 0].reshape(block_count, block_rows, local_heads, DH)
    starts = jnp.arange(block_count, dtype=jnp.int32) * block_rows
    key_index = jnp.arange(key_count, dtype=jnp.int32)
    in_span = key_index - past_len

    def scores(query_block, start):
        query_pos = start + jnp.arange(block_rows, dtype=jnp.int32)
        visible = jnp.where(
            key_index[None, :] < past_len,
            key_index[None, :] < offset,
            (in_span[None, :] <= query_pos[:, None]) & (in_span[None, :] < length),
        )
        raw_scores = (
            jnp.einsum("qhd,khd->hqk", query_block, all_keys, preferred_element_type=jnp.float32)
            * scale_factor
        )
        return jnp.where(visible[None], raw_scores, -jnp.inf)

    def backward_block(running, query_block, dout_block, masked):
        grad_keys, grad_values = running
        row_max = jnp.max(masked, axis=-1, keepdims=True)
        exp_terms = jnp.exp(masked - row_max)
        attention = exp_terms / jnp.sum(exp_terms, axis=-1, keepdims=True)
        attention_low = attention.astype(jnp.bfloat16)
        dprobs = jnp.einsum(
            "qhd,khd->hqk", dout_block, all_values, preferred_element_type=jnp.float32
        )
        row_delta = jnp.sum(attention * dprobs, axis=-1, keepdims=True)
        dscores = (attention * (dprobs - row_delta)).astype(jnp.bfloat16)
        grad_query = (
            jnp.einsum("hqk,khd->qhd", dscores, all_keys, preferred_element_type=jnp.float32)
            * scale_factor
        ).astype(jnp.bfloat16)
        grad_keys = (
            grad_keys
            + jnp.einsum("hqk,qhd->khd", dscores, query_block, preferred_element_type=jnp.float32)
            * scale_factor
        )
        grad_values = grad_values + jnp.einsum(
            "hqk,qhd->khd", attention_low, dout_block, preferred_element_type=jnp.float32
        )
        return ((grad_keys, grad_values), grad_query)

    zero_grads = (
        jnp.zeros((key_count, local_heads, DH), jnp.float32),
        jnp.zeros((key_count, local_heads, DH), jnp.float32),
    )
    rows_index = jnp.arange(span_len, dtype=jnp.int32)
    cleared = jnp.where(
        (rows_index < length)[:, None, None], head_dout[:, 0], jnp.zeros((), jnp.bfloat16)
    )
    dout_blocks = cleared.reshape(block_count, block_rows, local_heads, DH)

    def scan_step(running, scan_items):
        query_block, dout_block, start = scan_items
        return backward_block(running, query_block, dout_block, scores(query_block, start))

    (grad_keys, grad_values), grad_query = lax.scan(
        scan_step, zero_grads, (queries, dout_blocks, starts)
    )
    new_accum = past_accum[0] + jnp.stack([grad_keys[:past_len], grad_values[:past_len]], axis=1)
    span_grads = jnp.stack(
        [
            grad_query.reshape(span_len, local_heads, DH),
            grad_keys[past_len:].astype(jnp.bfloat16),
            grad_values[past_len:].astype(jnp.bfloat16),
        ],
        axis=1,
    )
    regrouped = lax.all_to_all(span_grads, "seq", split_axis=0, concat_axis=2, tiled=True)
    moved = from_behind(regrouped, "section", -1)
    return (moved.reshape(1, tok_rows, 3, HEADS * DH), new_accum[None])


def solution(mesh):
    in_specs = (
        P("section", "seq", None, None),
        P("section", "seq", None),
        P("section", None, None, "seq", None),
        P("section", None, None, "seq", None),
        P("section"),
        P("section"),
    )
    out_specs = (P("section", "seq", None, None), P("section", None, None, "seq", None))
    return jax.shard_map(
        per_device, mesh=mesh, in_specs=in_specs, out_specs=out_specs, check_vma=False
    )
```

profile of v0, /device:TPU:1, one launch (start us, length us, event | category | flops | bytes accessed | tf_op | source)
XLA Modules:
  0.0 325.4 jit_solution(9047187464734884413)
XLA Ops:
  0.6 1.3 copy.64
  1.9 1.1 copy.52
  3.1 13.0 %all-to-all-start.1 = ((bf16[32,1,64,128]{3,0,1,2:T(8,128)(2,1)}), bf16[32,1,64,128]{3,0,1,2:T(8,128)(2,1)S(1)}, u32[]{:S(2)}, u32[]{:S(2)}) async-start(bf16[32,1,64,128]{3,0,1,2:T(8,128)(2,1)} %copy.52), calls=%async_computation.1 | async-start | bytes 1048576 | tf_op jit(solution)/shard_map/all_to_all | solution.py:29
  16.5 2.2 copy.49
  18.6 15.1 %all-to-all-done.1 = bf16[32,1,64,128]{3,0,1,2:T(8,128)(2,1)S(1)} async-done(((bf16[32,1,64,128]{3,0,1,2:T(8,128)(2,1)}), bf16[32,1,64,128]{3,0,1,2:T(8,128)(2,1)S(1)}, u32[]{:S(2)}, u32[]{:S(2)}) %all-to-all-start.1) | async-done | bytes 524320 | tf_op jit(solution)/shard_map/all_to_all | solution.py:29
  33.7 0.8 copy-done.4
  34.6 5.9 %all-to-all-start = ((bf16[32,3,64,128]{3,0,1,2:T(8,128)(2,1)}), bf16[32,3,64,128]{3,0,1,2:T(8,128)(2,1)}, u32[]{:S(2)}, u32[]{:S(2)}) async-start(bf16[32,3,64,128]{3,0,1,2:T(8,128)(2,1)} %copy.49), calls=%async_computation | async-start | bytes 3145728 | tf_op jit(solution)/shard_map/all_to_all | solution.py:28
  40.4 2.7 copy.66
  43.9 0.9 broadcast_bitcast_fusion
  44.7 2.4 slice_bitcast_fusion
  47.1 2.2 select_bitcast_fusion
  49.3 30.1 %all-to-all-done = bf16[32,3,64,128]{3,0,1,2:T(8,128)(2,1)} async-done(((bf16[32,3,64,128]{3,0,1,2:T(8,128)(2,1)}), bf16[32,3,64,128]{3,0,1,2:T(8,128)(2,1)}, u32[]{:S(2)}, u32[]{:S(2)}) %all-to-all-start) | async-done | bytes 1572896 | tf_op jit(solution)/shard_map/all_to_all | solution.py:28
  79.4 1.8 copy.50
  81.2 0.9 slice_bitcast_fusion.2
  82.1 1.7 pad_maximum_fusion.1
  83.8 130.7 %while.16 = (s32[]{:T(128)}, f32[5120,1,128]{0,2,1:T(8,128)S(1)}, f32[5120,1,128]{0,2,1:T(8,128)}, bf16[4,512,1,128]{3,1,2,0:T(8,128)(2,1)}, bf16[4,512,1,128]{3...) while((s32[]{:T(128)}, f32[5120,1,128]{0,2,1:T(8,128)S(1)}, ...), condition=%wide.region_4.5_spmd.clone.clone, body=%wide.region_0.4_spmd.clone.clone.sunk | while | flops 3411304448 | bytes 200771376 | solution.py:95
  83.8 0.6 dynamic_slice.46
  85.0 1.3 iota_compare_fusion.4
  86.4 4.6 %fusion.62 = (f32[512]{0:T(512)S(1)}, f32[512,5120]{1,0:T(8,128)S(1)}) fusion(bf16[5120,1,128]{2,0,1:T(8,128)(2,1)} %get-tuple-element.356, bf16[4,512,1,128]{3,1,2,0:T(8,128)(2,1)} %get-tuple-element.352, s32[]{:T(128)} %get-tuple-element.335, pred[5120]{0:T(1024)(128)(4,1)S(1)} %get-tuple-element.316, s32[512]{0:T(512)S(1)} %iota_add_fusion.4, ...), kind=kOutput, calls=%fused_computation.57.clone.1 | convolution fusion | flops 686816768 | bytes 11968000 | tf_op jit(solution)/shard_map/while/body/eval_jaxpr/qhd,khd->hqk/dot_general | solution.py:51
  91.0 4.0 %copy-done = f32[512,5120]{1,0:T(8,128)} copy-done((f32[512,5120]{1,0:T(8,128)}, f32[512,5120]{1,0:T(8,128)S(1)}, u32[]{:S(2)}) %copy-start) | copy-done | bytes 10485784 | tf_op jit(solution)/shard_map/while
  94.9 1.6 fusion.63
  96.5 7.9 %fusion.65 = f32[5120,1,128]{0,2,1:T(8,128)} fusion(f32[5120,1,128]{0,2,1:T(8,128)} %get-tuple-element.337, pred[]{:T(512)S(6)} %compare.3, bf16[4,512,1,128]{3,1,2,0:T(8,128)(2,1)S(1)} %copy-done.9, s32[]{:T(128)} %get-tuple-element.335, f32[512,5120]{1,0:T(8,128)} %copy-done, f32[512]{0:T(512)S(1)} %fusion.63, f32[512]{0:T(512)S(1)} %get-tuple-element.319), kind=kOutput, calls=%fused_computation.11.clone.1 | convolution fusion | flops 680263680 | bytes 15863813 | tf_op jit(solution)/shard_map/while/body/eval_jaxpr/hqk,qhd->khd/dot_general | solution.py:76
  104.5 3.1 multiply_reduce_fusion.2
  107.6 3.6 %multiply_convert_fusion.2 = bf16[512,5120]{1,0:T(8,128)(2,1)S(1)} fusion(f32[512,5120]{1,0:T(8,128)S(1)} %get-tuple-element.320, f32[512]{0:T(512)S(1)} %get-tuple-element.321, f32[512]{0:T(512)S(1)} %fusion.63, f32[512,5120]{1,0:T(8,128)S(1)} %copy-done.1, f32[512]{0:T(512)S(1)} %get-tuple-element.319), kind=kLoop, calls=%fused_computation.2.clone.1 | loop fusion | flops 13107200 | bytes 26220544 | tf_op jit(solution)/shard_map/while/body/eval_jaxpr/convert_element_type | solution.py:66
  111.2 2.4 fusion.64
  113.7 2.2 fusion.66
  115.9 0.6 dynamic_slice.46
  117.1 1.3 iota_compare_fusion.4
  118.5 4.6 %fusion.62 = (f32[512]{0:T(512)S(1)}, f32[512,5120]{1,0:T(8,128)S(1)}) fusion(bf16[5120,1,128]{2,0,1:T(8,128)(2,1)} %get-tuple-element.356, bf16[4,512,1,128]{3,1,2,0:T(8,128)(2,1)} %get-tuple-element.352, s32[]{:T(128)} %get-tuple-element.335, pred[5120]{0:T(1024)(128)(4,1)S(1)} %get-tuple-element.316, s32[512]{0:T(512)S(1)} %iota_add_fusion.4, ...), kind=kOutput, calls=%fused_computation.57.clone.1 | convolution fusion | flops 686816768 | bytes 11968000 | tf_op jit(solution)/shard_map/while/body/eval_jaxpr/qhd,khd->hqk/dot_general | solution.py:51
  123.1 4.0 %copy-done = f32[512,5120]{1,0:T(8,128)} copy-done((f32[512,5120]{1,0:T(8,128)}, f32[512,5120]{1,0:T(8,128)S(1)}, u32[]{:S(2)}) %copy-start) | copy-done | bytes 10485784 | tf_op jit(solution)/shard_map/while
  127.1 1.6 fusion.63
  128.7 8.7 %fusion.65 = f32[5120,1,128]{0,2,1:T(8,128)} fusion(f32[5120,1,128]{0,2,1:T(8,128)} %get-tuple-element.337, pred[]{:T(512)S(6)} %compare.3, bf16[4,512,1,128]{3,1,2,0:T(8,128)(2,1)S(1)} %copy-done.9, s32[]{:T(128)} %get-tuple-element.335, f32[512,5120]{1,0:T(8,128)} %copy-done, f32[512]{0:T(512)S(1)} %fusion.63, f32[512]{0:T(512)S(1)} %get-tuple-element.319), kind=kOutput, calls=%fused_computation.11.clone.1 | convolution fusion | flops 680263680 | bytes 15863813 | tf_op jit(solution)/shard_map/while/body/eval_jaxpr/hqk,qhd->khd/dot_general | solution.py:76
  137.3 3.1 multiply_reduce_fusion.2
  140.5 3.6 %multiply_convert_fusion.2 = bf16[512,5120]{1,0:T(8,128)(2,1)S(1)} fusion(f32[512,5120]{1,0:T(8,128)S(1)} %get-tuple-element.320, f32[512]{0:T(512)S(1)} %get-tuple-element.321, f32[512]{0:T(512)S(1)} %fusion.63, f32[512,5120]{1,0:T(8,128)S(1)} %copy-done.1, f32[512]{0:T(512)S(1)} %get-tuple-element.319), kind=kLoop, calls=%fused_computation.2.clone.1 | loop fusion | flops 13107200 | bytes 26220544 | tf_op jit(solution)/shard_map/while/body/eval_jaxpr/convert_element_type | solution.py:66
  144.1 2.4 fusion.64
  146.6 2.2 fusion.66
  150.0 1.3 iota_compare_fusion.4
  151.3 4.6 %fusion.62 = (f32[512]{0:T(512)S(1)}, f32[512,5120]{1,0:T(8,128)S(1)}) fusion(bf16[5120,1,128]{2,0,1:T(8,128)(2,1)} %get-tuple-element.356, bf16[4,512,1,128]{3,1,2,0:T(8,128)(2,1)} %get-tuple-element.352, s32[]{:T(128)} %get-tuple-element.335, pred[5120]{0:T(1024)(128)(4,1)S(1)} %get-tuple-element.316, s32[512]{0:T(512)S(1)} %iota_add_fusion.4, ...), kind=kOutput, calls=%fused_computation.57.clone.1 | convolution fusion | flops 686816768 | bytes 11968000 | tf_op jit(solution)/shard_map/while/body/eval_jaxpr/qhd,khd->hqk/dot_general | solution.py:51
  155.9 4.0 %copy-done = f32[512,5120]{1,0:T(8,128)} copy-done((f32[512,5120]{1,0:T(8,128)}, f32[512,5120]{1,0:T(8,128)S(1)}, u32[]{:S(2)}) %copy-start) | copy-done | bytes 10485784 | tf_op jit(solution)/shard_map/while
  159.9 1.6 fusion.63
  161.5 8.7 %fusion.65 = f32[5120,1,128]{0,2,1:T(8,128)} fusion(f32[5120,1,128]{0,2,1:T(8,128)} %get-tuple-element.337, pred[]{:T(512)S(6)} %compare.3, bf16[4,512,1,128]{3,1,2,0:T(8,128)(2,1)S(1)} %copy-done.9, s32[]{:T(128)} %get-tuple-element.335, f32[512,5120]{1,0:T(8,128)} %copy-done, f32[512]{0:T(512)S(1)} %fusion.63, f32[512]{0:T(512)S(1)} %get-tuple-element.319), kind=kOutput, calls=%fused_computation.11.clone.1 | convolution fusion | flops 680263680 | bytes 15863813 | tf_op jit(solution)/shard_map/while/body/eval_jaxpr/hqk,qhd->khd/dot_general | solution.py:76
  170.2 3.1 multiply_reduce_fusion.2
  173.3 3.6 %multiply_convert_fusion.2 = bf16[512,5120]{1,0:T(8,128)(2,1)S(1)} fusion(f32[512,5120]{1,0:T(8,128)S(1)} %get-tuple-element.320, f32[512]{0:T(512)S(1)} %get-tuple-element.321, f32[512]{0:T(512)S(1)} %fusion.63, f32[512,5120]{1,0:T(8,128)S(1)} %copy-done.1, f32[512]{0:T(512)S(1)} %get-tuple-element.319), kind=kLoop, calls=%fused_computation.2.clone.1 | loop fusion | flops 13107200 | bytes 26220544 | tf_op jit(solution)/shard_map/while/body/eval_jaxpr/convert_element_type | solution.py:66
  177.0 2.4 fusion.64
  179.4 2.2 fusion.66
  182.9 1.3 iota_compare_fusion.4
  184.2 4.6 %fusion.62 = (f32[512]{0:T(512)S(1)}, f32[512,5120]{1,0:T(8,128)S(1)}) fusion(bf16[5120,1,128]{2,0,1:T(8,128)(2,1)} %get-tuple-element.356, bf16[4,512,1,128]{3,1,2,0:T(8,128)(2,1)} %get-tuple-element.352, s32[]{:T(128)} %get-tuple-element.335, pred[5120]{0:T(1024)(128)(4,1)S(1)} %get-tuple-element.316, s32[512]{0:T(512)S(1)} %iota_add_fusion.4, ...), kind=kOutput, calls=%fused_computation.57.clone.1 | convolution fusion | flops 686816768 | bytes 11968000 | tf_op jit(solution)/shard_map/while/body/eval_jaxpr/qhd,khd->hqk/dot_general | solution.py:51
  188.8 4.0 %copy-done = f32[512,5120]{1,0:T(8,128)} copy-done((f32[512,5120]{1,0:T(8,128)}, f32[512,5120]{1,0:T(8,128)S(1)}, u32[]{:S(2)}) %copy-start) | copy-done | bytes 10485784 | tf_op jit(solution)/shard_map/while
  192.8 1.6 fusion.63
  194.4 8.7 %fusion.65 = f32[5120,1,128]{0,2,1:T(8,128)} fusion(f32[5120,1,128]{0,2,1:T(8,128)} %get-tuple-element.337, pred[]{:T(512)S(6)} %compare.3, bf16[4,512,1,128]{3,1,2,0:T(8,128)(2,1)S(1)} %copy-done.9, s32[]{:T(128)} %get-tuple-element.335, f32[512,5120]{1,0:T(8,128)} %copy-done, f32[512]{0:T(512)S(1)} %fusion.63, f32[512]{0:T(512)S(1)} %get-tuple-element.319), kind=kOutput, calls=%fused_computation.11.clone.1 | convolution fusion | flops 680263680 | bytes 15863813 | tf_op jit(solution)/shard_map/while/body/eval_jaxpr/hqk,qhd->khd/dot_general | solution.py:76
  203.0 3.1 multiply_reduce_fusion.2
  206.2 3.6 %multiply_convert_fusion.2 = bf16[512,5120]{1,0:T(8,128)(2,1)S(1)} fusion(f32[512,5120]{1,0:T(8,128)S(1)} %get-tuple-element.320, f32[512]{0:T(512)S(1)} %get-tuple-element.321, f32[512]{0:T(512)S(1)} %fusion.63, f32[512,5120]{1,0:T(8,128)S(1)} %copy-done.1, f32[512]{0:T(512)S(1)} %get-tuple-element.319), kind=kLoop, calls=%fused_computation.2.clone.1 | loop fusion | flops 13107200 | bytes 26220544 | tf_op jit(solution)/shard_map/while/body/eval_jaxpr/convert_element_type | solution.py:66
  209.8 2.4 fusion.64
  212.3 2.2 fusion.66
  214.5 2.1 copy.56
  216.5 2.1 fusion.40
  218.6 2.2 copy.57
  220.9 1.2 pad_maximum_fusion
  222.1 10.0 %copy.58 = bf16[2048,3,1,128]{3,1,2,0:T(4,128)(2,1)S(1)} copy(bf16[2048,3,1,128]{3,0,2,1:T(8,128)(2,1)S(1)} %pad_maximum_fusion) | data formatting | bytes 3145728 | tf_op jit(solution)/shard_map/stack | solution.py:99
  232.1 55.9 %all_to_all.51 = bf16[2048,3,1,128]{3,1,2,0:T(4,128)(2,1)S(1)} all-to-all(bf16[2048,3,1,128]{3,1,2,0:T(4,128)(2,1)S(1)} %copy.58), channel_id=1, replica_groups=mesh['section'=4,'seq'=64] {'seq'}, dimensions={0} | all-to-all | bytes 3145728 | tf_op jit(solution)/shard_map/all_to_all | solution.py:107
  288.2 2.8 collective-permute-start
  291.2 5.1 %maximum_add_fusion = f32[1,3072,2,1,128]{4,3,2,1,0:T(1,128)} fusion(f32[1,3072,2,1,128]{4,3,2,1,0:T(1,128)S(1)} %copy-done.3, f32[1,3072,1,1,128]{4,3,2,1,0:T(1,128)S(1)} %bitcast.146, f32[1,3072,1,1,128]{4,3,2,1,0:T(1,128)S(1)} %bitcast.143), kind=kLoop, calls=%fused_computation.40 | loop fusion | flops 1572864 | bytes 9437184 | tf_op jit(solution)/shard_map/add | solution.py:98
  296.2 26.5 %collective-permute-done = bf16[32,3,64,128]{3,0,2,1:T(8,128)(2,1)S(1)} collective-permute-done((bf16[32,3,64,128]{3,0,2,1:T(8,128)(2,1)S(1)}, bf16[32,3,64,128]{3,0,2,1:T(8,128)(2,1)S(1)}, u32[]{:S(2)}, u32[]{:S(2)}) %collective-permute-start) | collective-permute-done | bytes 1572896 | tf_op jit(solution)/shard_map/ppermute | solution.py:15
  323.3 2.1 reshape.128
  (70 shorter events, 5.3 us)
Async XLA Ops:
  0.6 15.4 %copy-start.6 = (bf16[1,32,3,8192]{3,1,2,0:T(8,128)(2,1)S(1)}, bf16[1,32,3,8192]{3,1,2,0:T(8,128)(2,1)}, u32[]{:S(2)}) copy-start(bf16[1,32,3,8192]{3,1,2,0:T(8,128)(2,1)} %param.8) | copy-start | bytes 4718596
  3.1 30.7 %all-to-all-start.1 = ((bf16[32,1,64,128]{3,0,1,2:T(8,128)(2,1)}), bf16[32,1,64,128]{3,0,1,2:T(8,128)(2,1)S(1)}, u32[]{:S(2)}, u32[]{:S(2)}) async-start(bf16[32,1,64,128]{3,0,1,2:T(8,128)(2,1)} %copy.52), calls=%async_computation.1 | async-start | bytes 1048576 | tf_op jit(solution)/shard_map/all_to_all | solution.py:29
  33.7 0.8 copy-start.4
  34.6 44.9 %all-to-all-start = ((bf16[32,3,64,128]{3,0,1,2:T(8,128)(2,1)}), bf16[32,3,64,128]{3,0,1,2:T(8,128)(2,1)}, u32[]{:S(2)}, u32[]{:S(2)}) async-start(bf16[32,3,64,128]{3,0,1,2:T(8,128)(2,1)} %copy.49), calls=%async_computation | async-start | bytes 3145728 | tf_op jit(solution)/shard_map/all_to_all | solution.py:28
  79.4 2.7 copy-start.2
  90.9 4.0 %copy-start = (f32[512,5120]{1,0:T(8,128)}, f32[512,5120]{1,0:T(8,128)S(1)}, u32[]{:S(2)}) copy-start(f32[512,5120]{1,0:T(8,128)S(1)} %get-tuple-element.318) | copy-start | bytes 31457284 | tf_op jit(solution)/shard_map/while
  94.9 1.6 copy-start.9
  96.5 7.9 %copy-start.1 = (f32[512,5120]{1,0:T(8,128)S(1)}, f32[512,5120]{1,0:T(8,128)}, u32[]{:S(2)}) copy-start(f32[512,5120]{1,0:T(8,128)} %copy-done) | copy-start | bytes 31457284 | tf_op jit(solution)/shard_map/while
  96.5 7.9 %copy-start.8 = (bf16[5120,1,128]{2,0,1:T(8,128)(2,1)S(1)}, bf16[5120,1,128]{2,0,1:T(8,128)(2,1)}, u32[]{:S(2)}) copy-start(bf16[5120,1,128]{2,0,1:T(8,128)(2,1)} %get-tuple-element.358) | copy-start | bytes 3932164 | tf_op jit(solution)/shard_map/while
  111.2 2.5 copy-start.7
  123.1 4.0 %copy-start = (f32[512,5120]{1,0:T(8,128)}, f32[512,5120]{1,0:T(8,128)S(1)}, u32[]{:S(2)}) copy-start(f32[512,5120]{1,0:T(8,128)S(1)} %get-tuple-element.318) | copy-start | bytes 31457284 | tf_op jit(solution)/shard_map/while
  127.1 1.6 copy-start.9
  128.6 8.7 %copy-start.1 = (f32[512,5120]{1,0:T(8,128)S(1)}, f32[512,5120]{1,0:T(8,128)}, u32[]{:S(2)}) copy-start(f32[512,5120]{1,0:T(8,128)} %copy-done) | copy-start | bytes 31457284 | tf_op jit(solution)/shard_map/while
  128.7 8.7 %copy-start.8 = (bf16[5120,1,128]{2,0,1:T(8,128)(2,1)S(1)}, bf16[5120,1,128]{2,0,1:T(8,128)(2,1)}, u32[]{:S(2)}) copy-start(bf16[5120,1,128]{2,0,1:T(8,128)(2,1)} %get-tuple-element.358) | copy-start | bytes 3932164 | tf_op jit(solution)/shard_map/while
  144.1 2.5 copy-start.7
  155.9 4.0 %copy-start = (f32[512,5120]{1,0:T(8,128)}, f32[512,5120]{1,0:T(8,128)S(1)}, u32[]{:S(2)}) copy-start(f32[512,5120]{1,0:T(8,128)S(1)} %get-tuple-element.318) | copy-start | bytes 31457284 | tf_op jit(solution)/shard_map/while
  159.9 1.6 copy-start.9
  161.5 8.7 %copy-start.1 = (f32[512,5120]{1,0:T(8,128)S(1)}, f32[512,5120]{1,0:T(8,128)}, u32[]{:S(2)}) copy-start(f32[512,5120]{1,0:T(8,128)} %copy-done) | copy-start | bytes 31457284 | tf_op jit(solution)/shard_map/while
  161.5 8.7 %copy-start.8 = (bf16[5120,1,128]{2,0,1:T(8,128)(2,1)S(1)}, bf16[5120,1,128]{2,0,1:T(8,128)(2,1)}, u32[]{:S(2)}) copy-start(bf16[5120,1,128]{2,0,1:T(8,128)(2,1)} %get-tuple-element.358) | copy-start | bytes 3932164 | tf_op jit(solution)/shard_map/while
  176.9 2.5 copy-start.7
  188.8 4.0 %copy-start = (f32[512,5120]{1,0:T(8,128)}, f32[512,5120]{1,0:T(8,128)S(1)}, u32[]{:S(2)}) copy-start(f32[512,5120]{1,0:T(8,128)S(1)} %get-tuple-element.318) | copy-start | bytes 31457284 | tf_op jit(solution)/shard_map/while
  192.8 1.6 copy-start.9
  194.4 8.7 %copy-start.1 = (f32[512,5120]{1,0:T(8,128)S(1)}, f32[512,5120]{1,0:T(8,128)}, u32[]{:S(2)}) copy-start(f32[512,5120]{1,0:T(8,128)} %copy-done) | copy-start | bytes 31457284 | tf_op jit(solution)/shard_map/while
  194.4 8.7 %copy-start.8 = (bf16[5120,1,128]{2,0,1:T(8,128)(2,1)S(1)}, bf16[5120,1,128]{2,0,1:T(8,128)(2,1)}, u32[]{:S(2)}) copy-start(bf16[5120,1,128]{2,0,1:T(8,128)(2,1)} %get-tuple-element.358) | copy-start | bytes 3932164 | tf_op jit(solution)/shard_map/while
  209.8 2.5 copy-start.7
  218.6 2.3 copy-start.5
  288.2 2.9 slice-start
  288.2 2.9 copy-start.3
  288.2 34.5 %collective-permute-start = (bf16[32,3,64,128]{3,0,2,1:T(8,128)(2,1)S(1)}, bf16[32,3,64,128]{3,0,2,1:T(8,128)(2,1)S(1)}, u32[]{:S(2)}, u32[]{:S(2)}) collective-permute-start(bf16[32,3,64,128]{3,0,2,1:T(8,128)(2,1)S(1)} %bitcast.152), channel_id=1, source_target_pairs={{64,0},{128,64},{192,128},{0,192},{65,1},{129,65},{193,129},{1,193... | collective-permute-start | bytes 4718600 | tf_op jit(solution)/shard_map/ppermute | solution.py:15
where the time goes:
time: 329 us; the launch traced here: 325 us
  matrix products  83.2 us (25%)
  waiting for transfers between devices  71.7 us (22%)
  blocking collectives  55.9 us (17%)
  local copies, waits for them, and re-layouts  52.5 us (16%)
  other arithmetic  38.6 us (12%)
  starting transfers between devices  21.6 us (7%)
    all_to_all x1, blocking collectives, per_device(): lax.all_to_all(span_grads, 'seq', split_axis=0, concat_axis=2, tiled=True)  55.9 us
    dot_general x4, matrix products, backward_block(): jnp.einsum('hqk,qhd->khd', attention_low, dout_block, preferred_element_t...  33.9 us
    all_to_all x1, waiting for transfers between devices, per_device(): lax.all_to_all(local_rows, 'seq', split_axis=2, concat_axis=0, tiled=True)  30.1 us
    ppermute x1, waiting for transfers between devices, from_behind(): return lax.ppermute(block, axis, route)  26.5 us
    dot_general x4, matrix products, scores(): jnp.einsum('qhd,khd->hqk', query_block, all_keys, preferred_element_type=...  18.3 us
    while x40, local copies, waits for them, and re-layouts  16 us
    all_to_all x1, waiting for transfers between devices, per_device(): lax.all_to_all(upstream, 'seq', split_axis=2, concat_axis=0, tiled=True)  15.1 us
    convert_element_type x4, other arithmetic, backward_block(): dscores = (attention * (dprobs - row_delta)).astype(jnp.bfloat16)  14.5 us
  transfers between devices with their start and end apart: 3, of which 3 were waited for; matrix products, arithmetic and copies ran while one was open for 5% of the time, Pallas kernels for 0%

commit v1 on v0

v1 whole, which is shorter than its diff:
```python
import functools
import math

import jax
import jax.numpy as jnp
from jax import lax
from jax.experimental import pallas as pl
from jax.experimental.pallas import tpu as pltpu
from jax.sharding import PartitionSpec as P

HEADS = 64
DH = 128
NEG = -1e30
SCALE = 1.0 / math.sqrt(DH)
SCALE_LOG2 = SCALE * math.log2(math.e)
F32 = jnp.float32
BF16 = jnp.bfloat16
BQ = 512
BK = 1024
BS = 512


def pack_kernel(x_ref, g_ref, o_ref):
    for h in range(o_ref.shape[0]):
        cols = slice(h * DH, (h + 1) * DH)
        for p in range(3):
            o_ref[h, p] = x_ref[p, :, cols]
        o_ref[h, 3] = g_ref[:, cols]


def pack(x, g, heads_per_step=16):
    rows = x.shape[1]
    w = heads_per_step * DH
    return pl.pallas_call(
        pack_kernel,
        out_shape=jax.ShapeDtypeStruct((HEADS, 4, rows, DH), BF16),
        grid=(HEADS // heads_per_step,),
        in_specs=[
            pl.BlockSpec((3, rows, w), lambda i: (0, 0, i)),
            pl.BlockSpec((rows, w), lambda i: (0, i)),
        ],
        out_specs=pl.BlockSpec((heads_per_step, 4, rows, DH), lambda i: (i, 0, 0, 0)),
        name="pack",
    )(x, g)


def unpack_kernel(x_ref, o_ref):
    for h in range(x_ref.shape[0]):
        for p in range(x_ref.shape[1]):
            o_ref[p, :, h * DH : (h + 1) * DH] = x_ref[h, p]


def unpack(x, heads_per_step=16):
    planes, rows = x.shape[1], x.shape[2]
    return pl.pallas_call(
        unpack_kernel,
        out_shape=jax.ShapeDtypeStruct((planes, rows, HEADS * DH), BF16),
        grid=(HEADS // heads_per_step,),
        in_specs=[pl.BlockSpec((heads_per_step, planes, rows, DH), lambda i: (i, 0, 0, 0))],
        out_specs=pl.BlockSpec((planes, rows, heads_per_step * DH), lambda i: (0, 0, i)),
        name="unpack",
    )(x)


def attn_kernel(past, span, tok, sref, x_ref, pk_ref, pv_ref, acc_ref, og_ref, nacc_ref, s_sc, dp_sc, dka, dva):
    i = pl.program_id(0)
    nq = span // BQ
    offset = sref[0]
    length = sref[1]
    n_past = (offset + BK - 1) // BK

    @pl.when(i == 0)
    def _():
        dka[...] = jnp.zeros_like(dka)
        dva[...] = jnp.zeros_like(dva)

    def rows_of(plane, start, count):
        return x_ref[pl.ds(start // tok, count // tok), plane].reshape(count, DH)

    qstart = i * BQ
    dests = pl.ds(pl.multiple_of(qstart // tok, BQ // tok), BQ // tok)

    @pl.when(qstart >= length)
    def _():
        og_ref[dests, 0] = jnp.zeros((BQ // tok, tok, DH), BF16)

    @pl.when(qstart < length)
    def _():
        q = rows_of(0, qstart, BQ)
        g = rows_of(3, qstart, BQ)
        row = qstart + lax.broadcasted_iota(jnp.int32, (BQ, DH), 0)
        g = jnp.where(row < length, g, jnp.zeros_like(g))
        q_t = q.T
        g_t = g.T
        n_span = i + 1

        def fold(x, op):
            return op(x.reshape(x.shape[0] // 8, 8, BQ), axis=0)

        def score_past(b, m):
            r0 = pl.multiple_of(b * BK, BK)
            s = jnp.dot(pk_ref[pl.ds(r0, BK), :], q_t, preferred_element_type=F32)
            key = r0 + lax.broadcasted_iota(jnp.int32, (BK, BQ), 0)
            s = jnp.where(key < offset, s, NEG)
            s_sc[pl.ds(r0, BK), :] = s
            return jnp.maximum(m, fold(s, jnp.max))

        def score_span(b, m):
            r0 = pl.multiple_of(b * BS, BS)
            s = jnp.dot(rows_of(1, r0, BS), q_t, preferred_element_type=F32)
            key = r0 + lax.broadcasted_iota(jnp.int32, (BS, BQ), 0)
            query = qstart + lax.broadcasted_iota(jnp.int32, (BS, BQ), 1)
            s = jnp.where((key <= query) & (key < length), s, NEG)
            s_sc[pl.ds(pl.multiple_of(past + r0, BS), BS), :] = s
            return jnp.maximum(m, fold(s, jnp.max))

        m = lax.fori_loop(0, n_past, score_past, jnp.full((8, BQ), NEG, F32))
        m = lax.fori_loop(0, n_span, score_span, m)
        m_scaled = jnp.max(m, axis=0, keepdims=True) * SCALE_LOG2

        def stats(values, o0, size, carry):
            l, d = carry
            dp = jnp.dot(values, g_t, preferred_element_type=F32)
            e = jnp.exp2(s_sc[pl.ds(o0, size), :] * SCALE_LOG2 - m_scaled)
            s_sc[pl.ds(o0, size), :] = e
            dp_sc[pl.ds(o0, size), :] = dp
            return l + fold(e, jnp.sum), d + fold(e * dp, jnp.sum)

        def stats_past(b, carry):
            r0 = pl.multiple_of(b * BK, BK)
            return stats(pv_ref[pl.ds(r0, BK), :], r0, BK, carry)

        def stats_span(b, carry):
            r0 = pl.multiple_of(b * BS, BS)
            return stats(rows_of(2, r0, BS), pl.multiple_of(past + r0, BS), BS, carry)

        zero = jnp.zeros((8, BQ), F32)
        carry = lax.fori_loop(0, n_past, stats_past, (zero, zero))
        l, d = lax.fori_loop(0, n_span, stats_span, carry)
        inv_l = 1.0 / jnp.sum(l, axis=0, keepdims=True)
        delta = jnp.sum(d, axis=0, keepdims=True) * inv_l

        def grads(keys, o0, size, dq):
            p = s_sc[pl.ds(o0, size), :] * inv_l
            ds = (p * (dp_sc[pl.ds(o0, size), :] - delta)).astype(BF16)
            dva[pl.ds(o0, size), :] += jnp.dot(p.astype(BF16), g, preferred_element_type=F32)
            dka[pl.ds(o0, size), :] += jnp.dot(ds, q, preferred_element_type=F32)
            return dq + lax.dot_general(
                ds, keys, (((0,), (0,)), ((), ())), preferred_element_type=F32
            )

        def grads_past(b, dq):
            r0 = pl.multiple_of(b * BK, BK)
            return grads(pk_ref[pl.ds(r0, BK), :], r0, BK, dq)

        def grads_span(b, dq):
            r0 = pl.multiple_of(b * BS, BS)
            return grads(rows_of(1, r0, BS), pl.multiple_of(past + r0, BS), BS, dq)

        dq = lax.fori_loop(0, n_past, grads_past, jnp.zeros((BQ, DH), F32))
        dq = lax.fori_loop(0, n_span, grads_span, dq)
        og_ref[dests, 0] = (dq * SCALE).astype(BF16).reshape(BQ // tok, tok, DH)

    @pl.when(i == nq - 1)
    def _():
        n = span // tok
        og_ref[:, 1] = (dka[pl.ds(past, span), :] * SCALE).astype(BF16).reshape(n, tok, DH)
        og_ref[:, 2] = dva[pl.ds(past, span), :].astype(BF16).reshape(n, tok, DH)
        even = pl.ds(0, past, stride=2)
        odd = pl.ds(1, past, stride=2)
        nacc_ref[even, :] = acc_ref[even, :] + dka[pl.ds(0, past), :] * SCALE
        nacc_ref[odd, :] = acc_ref[odd, :] + dva[pl.ds(0, past), :]


def whole(shape):
    return pl.BlockSpec(shape, lambda i, s: (0,) * len(shape), pipeline_mode=pl.Buffered(1))


def attention_backward(bounds, x, past_k, past_v, accum):
    n, _, tok, _ = x.shape
    span, past = n * tok, past_k.shape[0]
    out_shape = (n, 3, tok, DH)
    return pl.pallas_call(
        functools.partial(attn_kernel, past, span, tok),
        out_shape=(jax.ShapeDtypeStruct(out_shape, BF16), jax.ShapeDtypeStruct(accum.shape, F32)),
        grid_spec=pltpu.PrefetchScalarGridSpec(
            num_scalar_prefetch=1,
            grid=(span // BQ,),
            in_specs=[whole(a.shape) for a in (x, past_k, past_v, accum)],
            out_specs=(whole(out_shape), whole(accum.shape)),
            scratch_shapes=[
                pltpu.VMEM((past + span, BQ), F32),
                pltpu.VMEM((past + span, BQ), F32),
                pltpu.VMEM((past + span, DH), F32),
                pltpu.VMEM((past + span, DH), F32),
            ],
        ),
        compiler_params=pltpu.CompilerParams(vmem_limit_bytes=56 * 2**20),
        name="attn_bwd",
    )(bounds, x, past_k, past_v, accum)


def from_behind(block, axis, distance):
    size = lax.axis_size(axis)
    return lax.ppermute(block, axis, [((i - distance) % size, i) for i in range(size)])


def per_device(span_inputs, out_grad, past_cache, past_accum, offsets, lengths):
    past = past_cache.shape[1]
    bounds = jnp.concatenate([offsets, lengths])
    packed = pack(jnp.transpose(span_inputs[0], (1, 0, 2)), out_grad[0])
    x = lax.all_to_all(packed, "seq", split_axis=0, concat_axis=0, tiled=True)
    cache = past_cache.reshape(past, 2, DH)
    grads, new_accum = attention_backward(
        bounds, x, cache[:, 0], cache[:, 1], past_accum.reshape(past * 2, DH)
    )
    y = lax.all_to_all(grads, "seq", split_axis=0, concat_axis=0, tiled=True)
    y = from_behind(y, "section", -1)
    out = jnp.transpose(unpack(y), (1, 0, 2))
    return out[None], new_accum.reshape(past_accum.shape)


def solution(mesh):
    in_specs = (
        P("section", "seq", None, None),
        P("section", "seq", None),
        P("section", None, None, "seq", None),
        P("section", None, None, "seq", None),
        P("section"),
        P("section"),
    )
    out_specs = (P("section", "seq", None, None), P("section", None, None, "seq", None))
    return jax.shard_map(
        per_device, mesh=mesh, in_specs=in_specs, out_specs=out_specs, check_vma=False
    )
```

time: 329 us -> 199 us (0.60)
  matrix products: 83.2 us -> 0 us
  Pallas kernels: 0 us -> 51.7 us
  local copies, waits for them, and re-layouts: 52.5 us -> 5.37 us
  other arithmetic: 38.6 us -> 0.59 us
  blocking collectives: 55.9 us -> 46 us
  starting transfers between devices: 21.6 us -> 13 us
  waiting for transfers between devices: 71.7 us -> 79.4 us
    dot_general x20 -> x0, matrix products: 83.2 us -> none  [the longest x4 33.9 us: backward_block(): jnp.einsum('hqk,qhd->khd', attention_low, dout_block, preferred_element_t...]
    pallas_call x0 -> x3, Pallas kernels: none -> 51.7 us  [the longest x1 44.2 us: attention_backward(): pl.pallas_call(functools.partial(attn_kernel, past, span, tok), out_shape...]
    while x42 -> x0, local copies, waits for them, and re-layouts: 20.3 us -> none
    another operation x5 -> x0, local copies, waits for them, and re-layouts: 15.4 us -> none  [the longest x3 12.1 us: per_device(): jnp.stack([grad_query.reshape(span_len, local_heads, DH), grad_keys[past_...]
    convert_element_type x4 -> x0, other arithmetic: 14.5 us -> none  [backward_block(): dscores = (attention * (dprobs - row_delta)).astype(jnp.bfloat16)]
    all_to_all x1, blocking collectives: 55.9 us -> 46 us  [per_device(): y = lax.all_to_all(grads, 'seq', split_axis=0, concat_axis=0, tiled=True)]
    ppermute x1, waiting for transfers between devices: 26.5 us -> 34.5 us  [from_behind(): lax.ppermute(block, axis, [((i - distance) % size, i) for i in range(size)])]
    add x5 -> x0, other arithmetic: 7.54 us -> none  [the longest x1 5.05 us: per_device(): past_accum[0]]
  transfers between devices with their start and end apart: 3 -> 2, of which waited for: 3 -> 2; matrix products, arithmetic and copies ran while one was open for 5% -> 2% of each run, Pallas kernels for 0% -> 0%
where the time goes in v1:
time: 199 us; the launch traced here: 198 us
  waiting for transfers between devices  79.4 us (40%)
  Pallas kernels  51.7 us (26%)
  blocking collectives  46 us (23%)
  starting transfers between devices  13 us (7%)
  local copies, waits for them, and re-layouts  5.37 us (3%)
    all_to_all x1, blocking collectives, per_device(): y = lax.all_to_all(grads, 'seq', split_axis=0, concat_axis=0, tiled=True)  46 us
    all_to_all x1, waiting for transfers between devices, per_device(): x = lax.all_to_all(packed, 'seq', split_axis=0, concat_axis=0, tiled=True)  44.9 us
    pallas_call x1, Pallas kernels, attention_backward(): pl.pallas_call(functools.partial(attn_kernel, past, span, tok), out_shape...  44.2 us
    ppermute x1, waiting for transfers between devices, from_behind(): lax.ppermute(block, axis, [((i - distance) % size, i) for i in range(size)])  34.5 us
    all_to_all x1, starting transfers between devices, per_device(): x = lax.all_to_all(packed, 'seq', split_axis=0, concat_axis=0, tiled=True)  13 us
    unnamed x5, local copies, waits for them, and re-layouts  4.12 us
  transfers between devices with their start and end apart: 2, of which 2 were waited for; matrix products, arithmetic and copies ran while one was open for 2% of the time, Pallas kernels for 0%

profile of v1, /device:TPU:1, one launch (start us, length us, event | category | flops | bytes accessed | tf_op | source)
XLA Modules:
  0.0 198.1 jit_solution(13597174569521441863)
XLA Ops:
  0.6 3.9 %pack.1 = bf16[64,4,32,128]{3,2,1,0:T(8,128)(2,1)} custom-call(bf16[3,32,8192]{2,1,0:T(8,128)(2,1)} %bitcast.21, bf16[32,8192]{1,0:T(8,128)(2,1)} %bitcast.22), custom_call_target="tpu_custom_call" | custom-call | tf_op jit(solution)/shard_map/pack/pallas_call | solution.py:34
  4.5 13.0 %all-to-all-start = ((bf16[64,4,32,128]{3,2,1,0:T(8,128)(2,1)}), bf16[64,4,32,128]{3,2,1,0:T(8,128)(2,1)S(1)}, u32[]{:S(2)}, u32[]{:S(2)}) async-start(bf16[64,4,32,128]{3,2,1,0:T(8,128)(2,1)} %pack.1), calls=%async_computation | async-start | bytes 4194304 | tf_op jit(solution)/shard_map/all_to_all | solution.py:212
  18.8 1.6 copy.11
  20.4 0.6 pad_add_fusion.sref
  21.0 1.3 slice_bitcast_fusion
  22.2 44.9 %all-to-all-done.x_ref = bf16[64,4,32,128]{3,2,1,0:T(8,128)(2,1)S(1)} async-done(((bf16[64,4,32,128]{3,2,1,0:T(8,128)(2,1)}), bf16[64,4,32,128]{3,2,1,0:T(8,128)(2,1)S(1)}, u32[]{:S(2)}, u32[]{:S(2)}) %all-to-all-start) | async-done | bytes 2097184 | tf_op jit(solution)/shard_map/all_to_all | solution.py:212
  67.2 0.0 copy-start
  67.2 1.4 copy-done
  68.5 44.2 %attn_bwd.1 = (bf16[64,3,32,128]{3,2,1,0:T(8,128)(2,1)}, f32[6144,128]{1,0:T(8,128)}) custom-call(s32[2]{0:T(128)} %pad_add_fusion.sref, bf16[64,4,32,128]{3,2,1,0:T(8,128)(2,1)} %copy-done, bf16[3072,128]{1,0:T(8,128)(2,1)} %get-tuple-element.9.pk_ref, bf16[3072,128]{1,0:T(8,128)(2,1)} %get-tuple-element.8.pv_ref, f32[6144,128]{1,0:T(8,128)} %bitcast.19), custom_call_target="tpu_custom_call" | custom-call | tf_op jit(solution)/shard_map/attn_bwd/pallas_call | solution.py:183
  112.7 46.0 %all_to_all.10 = bf16[64,3,32,128]{3,2,1,0:T(8,128)(2,1)S(1)} all-to-all(bf16[64,3,32,128]{3,2,1,0:T(8,128)(2,1)} %get-tuple-element.4), channel_id=1, replica_groups=mesh['section'=4,'seq'=64] {'seq'}, dimensions={0} | all-to-all | bytes 3145728 | tf_op jit(solution)/shard_map/all_to_all | solution.py:217
  158.7 0.0 collective-permute-start
  158.7 34.5 %collective-permute-done.x_ref = bf16[64,3,32,128]{3,2,1,0:T(8,128)(2,1)S(1)} collective-permute-done((bf16[64,3,32,128]{3,2,1,0:T(8,128)(2,1)S(1)}, bf16[64,3,32,128]{3,2,1,0:T(8,128)(2,1)S(1)}, u32[]{:S(2)}, u32[]{:S(2)}) %collective-permute-start) | collective-permute-done | bytes 1572896 | tf_op jit(solution)/shard_map/ppermute | solution.py:205
  193.2 0.0 copy-start.1
  193.2 1.2 copy-done.1
  194.4 3.7 %unpack.1 = bf16[3,32,8192]{2,1,0:T(8,128)(2,1)} custom-call(bf16[64,3,32,128]{3,2,1,0:T(8,128)(2,1)} %copy-done.1), custom_call_target="tpu_custom_call" | custom-call | tf_op jit(solution)/shard_map/unpack/pallas_call | solution.py:55
Async XLA Ops:
  4.5 62.7 %all-to-all-start = ((bf16[64,4,32,128]{3,2,1,0:T(8,128)(2,1)}), bf16[64,4,32,128]{3,2,1,0:T(8,128)(2,1)S(1)}, u32[]{:S(2)}, u32[]{:S(2)}) async-start(bf16[64,4,32,128]{3,2,1,0:T(8,128)(2,1)} %pack.1), calls=%async_computation | async-start | bytes 4194304 | tf_op jit(solution)/shard_map/all_to_all | solution.py:212
  67.2 1.4 copy-start
  158.7 34.5 %collective-permute-start = (bf16[64,3,32,128]{3,2,1,0:T(8,128)(2,1)S(1)}, bf16[64,3,32,128]{3,2,1,0:T(8,128)(2,1)S(1)}, u32[]{:S(2)}, u32[]{:S(2)}) collective-permute-start(bf16[64,3,32,128]{3,2,1,0:T(8,128)(2,1)S(1)} %all_to_all.10), channel_id=1, source_target_pairs={{64,0},{128,64},{192,128},{0,192},{65,1},{129,65},{193,129},{1,193... | collective-permute-start | bytes 4718600 | tf_op jit(solution)/shard_map/ppermute | solution.py:205
  193.2 1.2 copy-start.1

commit v2 on v1

v2 whole, which is shorter than its diff:
```python
import functools
import math

import jax
import jax.numpy as jnp
from jax import lax
from jax.experimental import pallas as pl
from jax.experimental.pallas import tpu as pltpu
from jax.sharding import PartitionSpec as P

HEADS = 64
DH = 128
NEG = -1e30
SCALE = 1.0 / math.sqrt(DH)
SCALE_LOG2 = SCALE * math.log2(math.e)
F32 = jnp.float32
BF16 = jnp.bfloat16
BQ = 512
BK = 1024
MIB = 2**20


def pack_kernel(x_ref, g_ref, o_ref):
    for h in range(o_ref.shape[0]):
        cols = slice(h * DH, (h + 1) * DH)
        for p in range(3):
            o_ref[h, p] = x_ref[p, :, cols]
        o_ref[h, 3] = g_ref[:, cols]


def pack(x, g, heads_per_step=16):
    rows = x.shape[1]
    w = heads_per_step * DH
    return pl.pallas_call(
        pack_kernel,
        out_shape=jax.ShapeDtypeStruct((HEADS, 4, rows, DH), BF16),
        grid=(HEADS // heads_per_step,),
        in_specs=[
            pl.BlockSpec((3, rows, w), lambda i: (0, 0, i)),
            pl.BlockSpec((rows, w), lambda i: (0, i)),
        ],
        out_specs=pl.BlockSpec((heads_per_step, 4, rows, DH), lambda i: (i, 0, 0, 0)),
        compiler_params=pltpu.CompilerParams(vmem_limit_bytes=62 * MIB),
        name="pack",
    )(x, g)


def unpack_kernel(q_ref, kv_ref, o_ref):
    for h in range(q_ref.shape[0]):
        cols = slice(h * DH, (h + 1) * DH)
        o_ref[0, :, cols] = q_ref[h]
        o_ref[1, :, cols] = kv_ref[h, 0]
        o_ref[2, :, cols] = kv_ref[h, 1]


def unpack(q, kv, heads_per_step=16):
    rows = q.shape[1]
    return pl.pallas_call(
        unpack_kernel,
        out_shape=jax.ShapeDtypeStruct((3, rows, HEADS * DH), BF16),
        grid=(HEADS // heads_per_step,),
        in_specs=[
            pl.BlockSpec((heads_per_step, rows, DH), lambda i: (i, 0, 0)),
            pl.BlockSpec((heads_per_step, 2, rows, DH), lambda i: (i, 0, 0, 0)),
        ],
        out_specs=pl.BlockSpec((3, rows, heads_per_step * DH), lambda i: (0, 0, i)),
        compiler_params=pltpu.CompilerParams(vmem_limit_bytes=16 * MIB),
        name="unpack",
    )(q, kv)


def whole(shape):
    return pl.BlockSpec(shape, lambda i, s: (0,) * len(shape), pipeline_mode=pl.Buffered(1))


def dot(a, b):
    return jnp.dot(a, b, preferred_element_type=F32)


def dot_rows(a, b):
    return lax.dot_general(a, b, (((0,), (0,)), ((), ())), preferred_element_type=F32)


def token_rows(x_ref, plane, start, count):
    tok = x_ref.shape[2]
    return x_ref[pl.ds(start // tok, count // tok), plane].reshape(count, DH)


def live_rows(g, start, length):
    row = start + lax.broadcasted_iota(jnp.int32, g.shape, 0)
    return jnp.where(row < length, g, jnp.zeros_like(g))


def fold(x, op):
    return op(x.reshape(x.shape[0] // 8, 8, x.shape[1]), axis=0)


def mask_past(s, r0, offset):
    key = r0 + lax.broadcasted_iota(jnp.int32, s.shape, 0)
    return jnp.where(key < offset, s, NEG)


def span_kernel(bounds, x_ref, pk_ref, pv_ref, okv_ref, dq_ref, stat_ref, s_sc, dp_sc, dka, dva):
    n, _, tok, _ = x_ref.shape
    i = pl.program_id(0)
    offset = bounds[0]
    length = bounds[1]
    qstart = i * BQ

    @pl.when(i == 0)
    def _():
        dka[...] = jnp.zeros_like(dka)
        dva[...] = jnp.zeros_like(dva)

    @pl.when(qstart >= length)
    def _():
        dq_ref[...] = jnp.zeros_like(dq_ref)
        stat_ref[...] = jnp.zeros_like(stat_ref)

    @pl.when(qstart < length)
    def _():
        q = token_rows(x_ref, 0, qstart, BQ)
        g = live_rows(token_rows(x_ref, 3, qstart, BQ), qstart, length)
        q_t = q.T
        g_t = g.T
        half = BQ // 2
        lo = pl.ds(pl.multiple_of(qstart, BQ), half)
        hi = pl.ds(pl.multiple_of(qstart + half, half), half)

        def update(s, dp, carry):
            m, l, d = carry
            m_new = jnp.maximum(m, jnp.max(fold(s, jnp.max), axis=0, keepdims=True))
            keep = jnp.exp2((m - m_new) * SCALE_LOG2)
            e = jnp.exp2(s * SCALE_LOG2 - m_new * SCALE_LOG2)
            return m_new, l * keep + fold(e, jnp.sum), d * keep + fold(e * dp, jnp.sum)

        def past_stats(b, carry, masked):
            r0 = pl.multiple_of(b * BK, BK)
            size = BK // 2
            parts = [pl.ds(r0 + k * size, size) for k in range(2)]
            s = [dot(pk_ref[r, :], q_t) for r in parts]
            dp = [dot(pv_ref[r, :], g_t) for r in parts]
            for k in range(2):
                if masked:
                    s[k] = mask_past(s[k], r0 + k * size, offset)
                carry = update(s[k], dp[k], carry)
            return carry

        def span_stats(b, carry):
            r0 = pl.multiple_of(b * BQ, BQ)
            s = dot(token_rows(x_ref, 1, r0, BQ), q_t)
            dp = dot(token_rows(x_ref, 2, r0, BQ), g_t)
            s_sc[pl.ds(r0, BQ), :] = s
            dp_sc[pl.ds(r0, BQ), :] = dp
            return update(s, dp, carry)

        def diagonal_stats(carry):
            key = lax.broadcasted_iota(jnp.int32, (half, BQ), 0)
            query = lax.broadcasted_iota(jnp.int32, (half, BQ), 1)
            s = dot(token_rows(x_ref, 1, qstart, half), q_t)
            dp = dot(token_rows(x_ref, 2, qstart, half), g_t)
            s_hi = dot(token_rows(x_ref, 1, qstart + half, half), q_t[:, half:])
            dp_hi = dot(token_rows(x_ref, 2, qstart + half, half), g_t[:, half:])
            s = jnp.where((key <= query) & (qstart + key < length), s, NEG)
            s_sc[lo, :] = s
            dp_sc[lo, :] = dp
            carry = update(s, dp, carry)
            key = key[:, :half]
            seen = (key <= query[:, :half]) & (qstart + half + key < length)
            s_hi = jnp.where(seen, s_hi, NEG)
            s_sc[hi, half:] = s_hi
            dp_sc[hi, half:] = dp_hi
            right = update(s_hi, dp_hi, tuple(c[:, half:] for c in carry))
            return tuple(jnp.concatenate([c[:, :half], r], axis=1) for c, r in zip(carry, right))

        zero = jnp.zeros((8, BQ), F32)
        carry = (jnp.full((1, BQ), NEG, F32), zero, zero)
        carry = lax.fori_loop(0, i, span_stats, carry)
        carry = diagonal_stats(carry)
        full = offset // BK
        carry = lax.fori_loop(0, full, functools.partial(past_stats, masked=False), carry)
        m, l, d = lax.fori_loop(
            full, (offset + BK - 1) // BK, functools.partial(past_stats, masked=True), carry
        )
        l = jnp.sum(l, axis=0, keepdims=True)
        delta = jnp.sum(d, axis=0, keepdims=True) / l
        lse = m * SCALE_LOG2 + jnp.log2(l)
        stat_ref[...] = jnp.concatenate([lse, delta, jnp.zeros((6, BQ), F32)], axis=0)

        def p_and_ds(rows, cols):
            p = jnp.exp2(s_sc[rows, cols] * SCALE_LOG2 - lse[:, cols])
            return p.astype(BF16), (p * (dp_sc[rows, cols] - delta[:, cols])).astype(BF16)

        def span_grads(b, dq):
            rows = pl.ds(pl.multiple_of(b * BQ, BQ), BQ)
            p, ds = p_and_ds(rows, slice(0, BQ))
            dva[rows, :] += dot(p, g)
            dka[rows, :] += dot(ds, q)
            return dq + dot_rows(ds, token_rows(x_ref, 1, b * BQ, BQ))

        dq = lax.fori_loop(0, i, span_grads, jnp.zeros((BQ, DH), F32))
        p, ds = p_and_ds(lo, slice(0, BQ))
        p_hi, ds_hi = p_and_ds(hi, slice(half, BQ))
        dva[lo, :] += dot(p, g)
        dka[lo, :] += dot(ds, q)
        dva[hi, :] += dot(p_hi, g[half:])
        dka[hi, :] += dot(ds_hi, q[half:])
        dq = dq + dot_rows(ds, token_rows(x_ref, 1, qstart, half))
        dq_ref[:half] = dq[:half]
        dq_ref[half:] = dq[half:] + dot_rows(ds_hi, token_rows(x_ref, 1, qstart + half, half))

    @pl.when(i == pl.num_programs(0) - 1)
    def _():
        okv_ref[:, 0] = (dka[...] * SCALE).astype(BF16).reshape(n, tok, DH)
        okv_ref[:, 1] = dva[...].astype(BF16).reshape(n, tok, DH)


def span_grads_and_stats(bounds, x, pk, pv):
    n, _, tok, _ = x.shape
    span = n * tok
    return pl.pallas_call(
        span_kernel,
        out_shape=(
            jax.ShapeDtypeStruct((n, 2, tok, DH), BF16),
            jax.ShapeDtypeStruct((span, DH), F32),
            jax.ShapeDtypeStruct((8, span), F32),
        ),
        grid_spec=pltpu.PrefetchScalarGridSpec(
            num_scalar_prefetch=1,
            grid=(span // BQ,),
            in_specs=[whole(a.shape) for a in (x, pk, pv)],
            out_specs=(
                whole((n, 2, tok, DH)),
                pl.BlockSpec((BQ, DH), lambda i, s: (i, 0)),
                pl.BlockSpec((8, BQ), lambda i, s: (0, i)),
            ),
            scratch_shapes=[
                pltpu.VMEM((span, BQ), F32),
                pltpu.VMEM((span, BQ), F32),
                pltpu.VMEM((span, DH), F32),
                pltpu.VMEM((span, DH), F32),
            ],
        ),
        compiler_params=pltpu.CompilerParams(vmem_limit_bytes=62 * MIB),
        cost_estimate=pl.CostEstimate(flops=7 * 10**9, bytes_accessed=6 * 10**6, transcendentals=10**7),
        name="attn_span",
    )(bounds, x, pk, pv)


def query_kernel(bounds, x_ref, pk_ref, pv_ref, dqs_ref, stat_ref, o_ref):
    tok = x_ref.shape[2]
    offset = bounds[0]
    length = bounds[1]
    qstart = pl.program_id(0) * BQ

    @pl.when(qstart >= length)
    def _():
        o_ref[...] = jnp.zeros_like(o_ref)

    @pl.when(qstart < length)
    def _():
        q_t = token_rows(x_ref, 0, qstart, BQ).T
        g_t = live_rows(token_rows(x_ref, 3, qstart, BQ), qstart, length).T
        lse = stat_ref[0:1]
        delta = stat_ref[1:2]

        def step(b, dq):
            r0 = pl.multiple_of(b * BK, BK)
            keys = pk_ref[pl.ds(r0, BK), :]
            p = jnp.exp2(mask_past(dot(keys, q_t), r0, offset) * SCALE_LOG2 - lse)
            dp = dot(pv_ref[pl.ds(r0, BK), :], g_t)
            ds = (p * (dp - delta)).astype(BF16)
            return dq + dot_rows(ds, keys)

        dq = lax.fori_loop(0, (offset + BK - 1) // BK, step, dqs_ref[...])
        o_ref[...] = (dq * SCALE).astype(BF16).reshape(BQ // tok, tok, DH)


def query_grads(bounds, x, pk, pv, dq_span, stats):
    n, _, tok, _ = x.shape
    span = n * tok
    return pl.pallas_call(
        query_kernel,
        out_shape=jax.ShapeDtypeStruct((n, tok, DH), BF16),
        grid_spec=pltpu.PrefetchScalarGridSpec(
            num_scalar_prefetch=1,
            grid=(span // BQ,),
            in_specs=[whole(a.shape) for a in (x, pk, pv)]
            + [
                pl.BlockSpec((BQ, DH), lambda i, s: (i, 0)),
                pl.BlockSpec((8, BQ), lambda i, s: (0, i)),
            ],
            out_specs=pl.BlockSpec((BQ // tok, tok, DH), lambda i, s: (i, 0, 0)),
        ),
        compiler_params=pltpu.CompilerParams(vmem_limit_bytes=62 * MIB),
        cost_estimate=pl.CostEstimate(flops=5 * 10**9, bytes_accessed=6 * 10**6, transcendentals=10**7),
        name="attn_query",
    )(bounds, x, pk, pv, dq_span, stats)


def past_kernel(first, bounds, x_ref, pk_ref, pv_ref, stat_ref, acc_ref, prev_ref, nacc_ref, dk, dv):
    del prev_ref
    offset = bounds[0]
    length = bounds[1]
    kstart = (first + pl.program_id(0)) * BK
    dk[...] = jnp.zeros_like(dk)
    dv[...] = jnp.zeros_like(dv)

    def step(i, carry):
        qstart = pl.multiple_of(i * BQ, BQ)
        q = token_rows(x_ref, 0, qstart, BQ)
        g = live_rows(token_rows(x_ref, 3, qstart, BQ), qstart, length)
        s = mask_past(dot(pk_ref[...], q.T), kstart, offset)
        p = jnp.exp2(s * SCALE_LOG2 - stat_ref[0:1, pl.ds(qstart, BQ)])
        dp = dot(pv_ref[...], g.T)
        ds = (p * (dp - stat_ref[1:2, pl.ds(qstart, BQ)])).astype(BF16)
        dk[...] += dot(ds, q)
        dv[...] += dot(p.astype(BF16), g)
        return carry

    @pl.when(kstart < offset)
    def _():
        lax.fori_loop(0, (length + BQ - 1) // BQ, step, 0)

    even = pl.ds(0, BK, stride=2)
    odd = pl.ds(1, BK, stride=2)
    nacc_ref[even, :] = acc_ref[even, :] + dk[...] * SCALE
    nacc_ref[odd, :] = acc_ref[odd, :] + dv[...]


def past_grads(bounds, x, pk, pv, stats, accum, first, count, prev=None):
    keys = pl.BlockSpec((BK, DH), lambda i, s: (first + i, 0))
    pairs = pl.BlockSpec((2 * BK, DH), lambda i, s: (first + i, 0))
    args = [bounds, x, pk, pv, stats, accum]
    in_specs = [whole(x.shape), keys, keys, whole(stats.shape), pairs]
    body = functools.partial(past_kernel, first)
    aliases = {}
    if prev is None:
        body = lambda *refs: past_kernel(first, *refs[:6], None, *refs[6:])
    else:
        args.append(prev)
        in_specs.append(pl.BlockSpec(memory_space=pl.ANY))
        aliases = {6: 0}
    return pl.pallas_call(
        body,
        out_shape=jax.ShapeDtypeStruct(accum.shape, F32),
        grid_spec=pltpu.PrefetchScalarGridSpec(
            num_scalar_prefetch=1,
            grid=(count,),
            in_specs=in_specs,
            out_specs=pairs,
            scratch_shapes=[pltpu.VMEM((BK, DH), F32), pltpu.VMEM((BK, DH), F32)],
        ),
        input_output_aliases=aliases,
        compiler_params=pltpu.CompilerParams(vmem_limit_bytes=62 * MIB),
        cost_estimate=pl.CostEstimate(
            flops=2 * 10**9 * count, bytes_accessed=4 * 10**6 * count, transcendentals=10**6 * count
        ),
        name=f"attn_past{first}",
    )(*args)


def to_heads(x):
    return lax.all_to_all(x, "seq", split_axis=0, concat_axis=0, tiled=True)


def from_behind(block, axis, distance):
    size = lax.axis_size(axis)
    return lax.ppermute(block, axis, [((i - distance) % size, i) for i in range(size)])


def per_device(span_inputs, out_grad, past_cache, past_accum, offsets, lengths):
    past = past_cache.shape[1]
    bounds = jnp.concatenate([offsets, lengths])
    cache = past_cache.reshape(past, 2, DH)
    pk, pv = cache[:, 0], cache[:, 1]
    x = to_heads(pack(jnp.transpose(span_inputs[0], (1, 0, 2)), out_grad[0]))
    kv, dq_span, stats = span_grads_and_stats(bounds, x, pk, pv)
    kv = to_heads(kv)
    dq = query_grads(bounds, x, pk, pv, dq_span, stats)
    dq, bounds = lax.optimization_barrier((dq, bounds))
    dq = from_behind(dq, "section", -1)
    accum = past_accum.reshape(past * 2, DH)
    new_accum = past_grads(bounds, x, pk, pv, stats, accum, 0, 1)
    kv, dq, new_accum, bounds = lax.optimization_barrier((kv, dq, new_accum, bounds))
    dq = to_heads(dq)
    kv = from_behind(kv, "section", -1)
    new_accum = past_grads(bounds, x, pk, pv, stats, accum, 1, past // BK - 1, new_accum)
    out = jnp.transpose(unpack(dq, kv), (1, 0, 2))
    return out[None], new_accum.reshape(past_accum.shape)


def solution(mesh):
    in_specs = (
        P("section", "seq", None, None),
        P("section", "seq", None),
        P("section", None, None, "seq", None),
        P("section", None, None, "seq", None),
        P("section"),
        P("section"),
    )
    out_specs = (P("section", "seq", None, None), P("section", None, None, "seq", None))
    return jax.shard_map(
        per_device, mesh=mesh, in_specs=in_specs, out_specs=out_specs, check_vma=False
    )
```

time: 199 us -> 165 us (0.83)
  blocking collectives: 46 us -> 0 us
  waiting for transfers between devices: 79.4 us -> 52.7 us
  Pallas kernels: 51.7 us -> 72.2 us
  starting transfers between devices: 13 us -> 33.2 us
  local copies, waits for them, and re-layouts: 5.37 us -> 2.25 us
    all_to_all x1 -> x0, blocking collectives: 46 us -> none  [per_device(): y = lax.all_to_all(grads, 'seq', split_axis=0, concat_axis=0, tiled=True)]
    ppermute x1 -> x2, waiting for transfers between devices: 34.5 us -> 3.86 us  [from_behind(): lax.ppermute(block, axis, [((i - distance) % size, i) for i in range(size)])]
    pallas_call x2 -> x5, Pallas kernels: 47.9 us -> 68.3 us  [the longest x1 24.9 us: span_grads_and_stats(): pl.pallas_call(span_kernel, out_shape=(jax.ShapeDtypeStruct((n, 2, tok, D...]
    all_to_all x1 -> x3, starting transfers between devices: 13 us -> 31.7 us  [to_heads(): return lax.all_to_all(x, 'seq', split_axis=0, concat_axis=0, tiled=True)]
    all_to_all x1 -> x3, waiting for transfers between devices: 44.9 us -> 48.8 us  [to_heads(): return lax.all_to_all(x, 'seq', split_axis=0, concat_axis=0, tiled=True)]
    unnamed x5, local copies, waits for them, and re-layouts: 4.12 us -> 1 us
  transfers between devices with their start and end apart: 2 -> 5, of which waited for: 2 -> 3; matrix products, arithmetic and copies ran while one was open for 2% -> 1% of each run, Pallas kernels for 0% -> 26%
where the time goes in v2:
time: 165 us; the launch traced here: 163 us
  Pallas kernels  72.2 us (44%)
  waiting for transfers between devices  52.7 us (32%)
  starting transfers between devices  33.2 us (20%)
  local copies, waits for them, and re-layouts  2.25 us (1%)
  between operations  1.97 us (1%)
    all_to_all x3, waiting for transfers between devices, to_heads(): return lax.all_to_all(x, 'seq', split_axis=0, concat_axis=0, tiled=True)  48.8 us
    all_to_all x3, starting transfers between devices, to_heads(): return lax.all_to_all(x, 'seq', split_axis=0, concat_axis=0, tiled=True)  31.7 us
    pallas_call x1, Pallas kernels, span_grads_and_stats(): pl.pallas_call(span_kernel, out_shape=(jax.ShapeDtypeStruct((n, 2, tok, D...  24.9 us
    pallas_call x2, Pallas kernels, past_grads(): pl.pallas_call(body, out_shape=jax.ShapeDtypeStruct(accum.shape, F32), gr...  24.5 us
    pallas_call x1, Pallas kernels, query_grads(): pl.pallas_call(query_kernel, out_shape=jax.ShapeDtypeStruct((n, tok, DH),...  17.1 us
    pallas_call x1, Pallas kernels, pack(): pl.pallas_call(pack_kernel, out_shape=jax.ShapeDtypeStruct((HEADS, 4, row...  3.86 us
    ppermute x2, waiting for transfers between devices, from_behind(): lax.ppermute(block, axis, [((i - distance) % size, i) for i in range(size)])  3.86 us
  transfers between devices with their start and end apart: 5, of which 3 were waited for; matrix products, arithmetic and copies ran while one was open for 1% of the time, Pallas kernels for 26%

profile of v2, /device:TPU:1, one launch (start us, length us, event | category | flops | bytes accessed | tf_op | source)
XLA Modules:
  0.0 162.9 jit_solution(1514439105877488436)
XLA Ops:
  0.6 3.9 %pack.1 = bf16[64,4,32,128]{3,2,1,0:T(8,128)(2,1)} custom-call(bf16[3,32,8192]{2,1,0:T(8,128)(2,1)} %bitcast.23, bf16[32,8192]{1,0:T(8,128)(2,1)} %bitcast.24), custom_call_target="tpu_custom_call" | custom-call | tf_op jit(solution)/shard_map/pack/pallas_call | solution.py:34
  4.5 0.0 copy-start
  4.5 13.3 %all-to-all-start = ((bf16[64,4,32,128]{3,2,1,0:T(8,128)(2,1)}), bf16[64,4,32,128]{3,2,1,0:T(8,128)(2,1)}, u32[]{:S(2)}, u32[]{:S(2)}) async-start(bf16[64,4,32,128]{3,2,1,0:T(8,128)(2,1)} %pack.1), calls=%async_computation | async-start | bytes 4194304 | tf_op jit(solution)/shard_map/all_to_all | solution.py:364
  19.1 0.0 copy-done
  19.1 0.2 copy.12
  19.3 0.6 pad_add_fusion.bounds.refs_0_
  19.9 1.3 slice_bitcast_fusion
  21.1 46.3 %all-to-all-done.x_ref.refs_1_ = bf16[64,4,32,128]{3,2,1,0:T(8,128)(2,1)} async-done(((bf16[64,4,32,128]{3,2,1,0:T(8,128)(2,1)}), bf16[64,4,32,128]{3,2,1,0:T(8,128)(2,1)}, u32[]{:S(2)}, u32[]{:S(2)}) %all-to-all-start) | async-done | bytes 2097184 | tf_op jit(solution)/shard_map/all_to_all | solution.py:364
  67.4 24.9 %attn_span.1 = (bf16[64,2,32,128]{3,2,1,0:T(8,128)(2,1)}, f32[2048,128]{1,0:T(8,128)}, f32[8,2048]{1,0:T(8,128)}) custom-call(s32[2]{0:T(128)} %pad_add_fusion.bounds.refs_0_, bf16[64,4,32,128]{3,2,1,0:T(8,128)(2,1)} %all-to-all-done.x_ref.refs_1_, bf16[3072,128]{1,0:T(8,128)(2,1)} %get-tuple-element.23.pk_ref.refs_2_, ...), custom_call_target="tpu_custom_call" | custom-call | flops 7000000000 | bytes 6000000 | tf_op jit(solution)/shard_map/attn_span/pallas_call | solution.py:221
  92.4 7.2 %all-to-all-start.1 = ((bf16[64,2,32,128]{3,2,1,0:T(8,128)(2,1)}), bf16[64,2,32,128]{3,2,1,0:T(8,128)(2,1)}, u32[]{:S(2)}, u32[]{:S(2)}) async-start(bf16[64,2,32,128]{3,2,1,0:T(8,128)(2,1)} %get-tuple-element.11), calls=%async_computation.1 | async-start | bytes 2097152 | tf_op jit(solution)/shard_map/all_to_all | solution.py:364
  99.5 17.1 %attn_query.1 = bf16[64,32,128]{2,1,0:T(8,128)(2,1)} custom-call(s32[2]{0:T(128)} %pad_add_fusion.bounds.refs_0_, bf16[64,4,32,128]{3,2,1,0:T(8,128)(2,1)} %all-to-all-done.x_ref.refs_1_, bf16[3072,128]{1,0:T(8,128)(2,1)} %get-tuple-element.23.pk_ref.refs_2_, bf16[3072,128]{1,0:T(8,128)(2,1)} %get-tuple-element.22.pv_ref.refs_3_, ...), custom_call_target="tpu_custom_call" | custom-call | flops 5000000000 | bytes 6000000 | tf_op jit(solution)/shard_map/attn_query/pallas_call | solution.py:282
  116.6 0.0 collective-permute-start
  116.6 9.3 %attn_past0.1.prev_ref = f32[6144,128]{1,0:T(8,128)} custom-call(s32[2]{0:T(128)} %pad_add_fusion.bounds.refs_0_, bf16[64,4,32,128]{3,2,1,0:T(8,128)(2,1)} %all-to-all-done.x_ref.refs_1_, bf16[3072,128]{1,0:T(8,128)(2,1)} %get-tuple-element.23.pk_ref.refs_2_, bf16[3072,128]{1,0:T(8,128)(2,1)} %get-tuple-element.22.pv_ref.refs_3_, ...), custom_call_target="tpu_custom_call" | custom-call | flops 2000000000 | bytes 4000000 | tf_op jit(solution)/shard_map/attn_past0/pallas_call | solution.py:344
  125.9 3.9 %collective-permute-done = bf16[64,32,128]{2,1,0:T(8,128)(2,1)S(1)} collective-permute-done((bf16[64,32,128]{2,1,0:T(8,128)(2,1)}, bf16[64,32,128]{2,1,0:T(8,128)(2,1)S(1)}, u32[]{:S(2)}, u32[]{:S(2)}) %collective-permute-start) | collective-permute-done | bytes 524320 | tf_op jit(solution)/shard_map/ppermute | solution.py:369
  129.8 0.0 copy-start.1
  129.8 0.0 all-to-all-done.1
  129.8 0.8 copy-done.1
  130.6 1.5 collective-permute-start.1
  132.1 11.3 %all-to-all-start.2 = ((bf16[64,32,128]{2,1,0:T(8,128)(2,1)}), bf16[64,32,128]{2,1,0:T(8,128)(2,1)S(1)}, u32[]{:S(2)}, u32[]{:S(2)}) async-start(bf16[64,32,128]{2,1,0:T(8,128)(2,1)} %copy-done.1), calls=%async_computation.2 | async-start | bytes 1048576 | tf_op jit(solution)/shard_map/all_to_all | solution.py:364
  143.4 15.1 %attn_past1.1 = f32[6144,128]{1,0:T(8,128)} custom-call(s32[2]{0:T(128)} %pad_add_fusion.bounds.refs_0_, bf16[64,4,32,128]{3,2,1,0:T(8,128)(2,1)} %all-to-all-done.x_ref.refs_1_, bf16[3072,128]{1,0:T(8,128)(2,1)} %get-tuple-element.23.pk_ref.refs_2_, bf16[3072,128]{1,0:T(8,128)(2,1)} %get-tuple-element.22.pv_ref.refs_3_, ...), custom_call_target="tpu_custom_call", output_to_operand_aliasing={{}: (6, {})} | custom-call | flops 4000000000 | bytes 8000000 | tf_op jit(solution)/shard_map/attn_past1/pallas_call | solution.py:344
  158.5 2.5 %all-to-all-done.2.q_ref = bf16[64,32,128]{2,1,0:T(8,128)(2,1)S(1)} async-done(((bf16[64,32,128]{2,1,0:T(8,128)(2,1)}), bf16[64,32,128]{2,1,0:T(8,128)(2,1)S(1)}, u32[]{:S(2)}, u32[]{:S(2)}) %all-to-all-start.2) | async-done | bytes 524320 | tf_op jit(solution)/shard_map/all_to_all | solution.py:364
  161.1 0.0 collective-permute-done.1.kv_ref
  161.1 1.8 %unpack.1 = bf16[3,32,8192]{2,1,0:T(8,128)(2,1)} custom-call(bf16[64,32,128]{2,1,0:T(8,128)(2,1)S(1)} %all-to-all-done.2.q_ref, bf16[64,2,32,128]{3,2,1,0:T(8,128)(2,1)S(1)} %collective-permute-done.1.kv_ref), custom_call_target="tpu_custom_call" | custom-call | tf_op jit(solution)/shard_map/unpack/pallas_call | solution.py:58
Async XLA Ops:
  4.5 14.6 %copy-start = (bf16[1,3072,2,1,128]{4,2,3,1,0:T(2,128)(2,1)S(1)}, bf16[1,3072,2,1,128]{4,2,3,1,0:T(2,128)(2,1)}, u32[]{:S(2)}) copy-start(bf16[1,3072,2,1,128]{4,2,3,1,0:T(2,128)(2,1)} %param.8) | copy-start | bytes 4718596
  4.5 62.9 %all-to-all-start = ((bf16[64,4,32,128]{3,2,1,0:T(8,128)(2,1)}), bf16[64,4,32,128]{3,2,1,0:T(8,128)(2,1)}, u32[]{:S(2)}, u32[]{:S(2)}) async-start(bf16[64,4,32,128]{3,2,1,0:T(8,128)(2,1)} %pack.1), calls=%async_computation | async-start | bytes 4194304 | tf_op jit(solution)/shard_map/all_to_all | solution.py:364
  92.4 37.4 %all-to-all-start.1 = ((bf16[64,2,32,128]{3,2,1,0:T(8,128)(2,1)}), bf16[64,2,32,128]{3,2,1,0:T(8,128)(2,1)}, u32[]{:S(2)}, u32[]{:S(2)}) async-start(bf16[64,2,32,128]{3,2,1,0:T(8,128)(2,1)} %get-tuple-element.11), calls=%async_computation.1 | async-start | bytes 2097152 | tf_op jit(solution)/shard_map/all_to_all | solution.py:364
  116.6 13.2 %collective-permute-start = (bf16[64,32,128]{2,1,0:T(8,128)(2,1)}, bf16[64,32,128]{2,1,0:T(8,128)(2,1)S(1)}, u32[]{:S(2)}, u32[]{:S(2)}) collective-permute-start(bf16[64,32,128]{2,1,0:T(8,128)(2,1)} %attn_query.1), channel_id=1, source_target_pairs={{64,0},{128,64},{192,128},{0,192},{65,1},{129,65},{193,129},{1,193... | collective-permute-start | bytes 1572872 | tf_op jit(solution)/shard_map/ppermute | solution.py:369
  129.8 0.8 copy-start.1
  130.6 30.5 %collective-permute-start.1 = (bf16[64,2,32,128]{3,2,1,0:T(8,128)(2,1)}, bf16[64,2,32,128]{3,2,1,0:T(8,128)(2,1)S(1)}, u32[]{:S(2)}, u32[]{:S(2)}) collective-permute-start(bf16[64,2,32,128]{3,2,1,0:T(8,128)(2,1)} %all-to-all-done.1), channel_id=1, source_target_pairs={{64,0},{128,64},{192,128},{0,192},{65,1},{129,65},{193,129},{1,193... | collective-permute-start | bytes 3145736 | tf_op jit(solution)/shard_map/ppermute | solution.py:369
  132.1 29.0 %all-to-all-start.2 = ((bf16[64,32,128]{2,1,0:T(8,128)(2,1)}), bf16[64,32,128]{2,1,0:T(8,128)(2,1)S(1)}, u32[]{:S(2)}, u32[]{:S(2)}) async-start(bf16[64,32,128]{2,1,0:T(8,128)(2,1)} %copy-done.1), calls=%async_computation.2 | async-start | bytes 1048576 | tf_op jit(solution)/shard_map/all_to_all | solution.py:364

commit v3 on v2

--- a/solution.py
+++ b/solution.py
@@ -20,26 +20,49 @@
 MIB = 2**20
 
 
-def pack_kernel(x_ref, g_ref, o_ref):
-    for h in range(o_ref.shape[0]):
-        cols = slice(h * DH, (h + 1) * DH)
-        for p in range(3):
-            o_ref[h, p] = x_ref[p, :, cols]
-        o_ref[h, 3] = g_ref[:, cols]
-
-
-def pack(x, g, heads_per_step=16):
-    rows = x.shape[1]
-    w = heads_per_step * DH
+def pack_kernel(chunks, x_hbm, g_hbm, o_hbm, x_ref, g_ref, o_ref, in_sem, out_sem):
+    heads = HEADS // chunks
+    copies = []
+    for c in range(chunks):
+        cols = pl.ds(c * heads * DH, heads * DH)
+        copies.append((
+            pltpu.make_async_copy(x_hbm.at[:, :, cols], x_ref.at[:, :, cols], in_sem.at[0, c]),
+            pltpu.make_async_copy(g_hbm.at[:, cols], g_ref.at[:, cols], in_sem.at[1, c]),
+        ))
+    for pair in copies:
+        for copy in pair:
+            copy.start()
+    stores = []
+    for c in range(chunks):
+        for copy in copies[c]:
+            copy.wait()
+        for h in range(c * heads, (c + 1) * heads):
+            cols = slice(h * DH, (h + 1) * DH)
+            for p in range(3):
+                o_ref[h, p] = x_ref[p, :, cols]
+            o_ref[h, 3] = g_ref[:, cols]
+        rows = pl.ds(c * heads, heads)
+        stores.append(pltpu.make_async_copy(o_ref.at[rows], o_hbm.at[rows], out_sem.at[c]))
+        stores[-1].start()
+    for store in stores:
+        store.wait()
+
+
+def pack(x, g, chunks=8):
+    shape = (HEADS, 4, x.shape[1], DH)
+    hbm = pl.BlockSpec(memory_space=pl.ANY)
     return pl.pallas_call(
-        pack_kernel,
-        out_shape=jax.ShapeDtypeStruct((HEADS, 4, rows, DH), BF16),
-        grid=(HEADS // heads_per_step,),
-        in_specs=[
-            pl.BlockSpec((3, rows, w), lambda i: (0, 0, i)),
-            pl.BlockSpec((rows, w), lambda i: (0, i)),
+        functools.partial(pack_kernel, chunks),
+        out_shape=jax.ShapeDtypeStruct(shape, BF16),
+        in_specs=[hbm, hbm],
+        out_specs=hbm,
+        scratch_shapes=[
+            pltpu.VMEM(x.shape, BF16),
+            pltpu.VMEM(g.shape, BF16),
+            pltpu.VMEM(shape, BF16),
+            pltpu.SemaphoreType.DMA((2, chunks)),
+            pltpu.SemaphoreType.DMA((chunks,)),
         ],
-        out_specs=pl.BlockSpec((heads_per_step, 4, rows, DH), lambda i: (i, 0, 0, 0)),
         compiler_params=pltpu.CompilerParams(vmem_limit_bytes=62 * MIB),
         name="pack",
     )(x, g)
@@ -100,22 +123,66 @@
     return jnp.where(key < offset, s, NEG)
 
 
-def span_kernel(bounds, x_ref, pk_ref, pv_ref, okv_ref, dq_ref, stat_ref, s_sc, dp_sc, dka, dva):
+def past_copies(pk_hbm, pv_hbm, pk_ref, pv_ref, sems, b):
+    rows = pl.ds(pl.multiple_of(b * BK, BK), BK)
+    return (
+        pltpu.make_async_copy(pk_hbm.at[rows], pk_ref.at[rows], sems.at[0, b]),
+        pltpu.make_async_copy(pv_hbm.at[rows], pv_ref.at[rows], sems.at[1, b]),
+    )
+
+
+def each(count, action):
+    def body(b, carry):
+        action(b)
+        return carry
+
+    lax.fori_loop(0, count, body, 0)
+
+
+def span_kernel(
+    bounds, x_hbm, pk_hbm, pv_hbm, okv_ref, dq_ref, stat_ref,
+    x_ref, pk_ref, pv_ref, s_sc, dp_sc, dka, dva, x_sem, past_sem,
+):
     n, _, tok, _ = x_ref.shape
     i = pl.program_id(0)
     offset = bounds[0]
     length = bounds[1]
     qstart = i * BQ
+    n_past = (offset + BK - 1) // BK
+
+    def x_copy(c):
+        rows = pl.ds(c * (BQ // tok), BQ // tok)
+        return pltpu.make_async_copy(x_hbm.at[rows], x_ref.at[rows], x_sem.at[c])
+
+    def start_past(b):
+        for copy in past_copies(pk_hbm, pv_hbm, pk_ref, pv_ref, past_sem, b):
+            copy.start()
+
+    def wait_past(b):
+        @pl.when(i == 0)
+        def _():
+            for copy in past_copies(pk_hbm, pv_hbm, pk_ref, pv_ref, past_sem, b):
+                copy.wait()
+
+    @pl.when(i == 0)
+    def _():
+        x_copy(0).start()
+        each(n_past, start_past)
+        for c in range(1, n * tok // BQ):
+            x_copy(c).start()
 
     @pl.when(i == 0)
     def _():
         dka[...] = jnp.zeros_like(dka)
         dva[...] = jnp.zeros_like(dva)
 
+    x_copy(i).wait()
+
     @pl.when(qstart >= length)
     def _():
         dq_ref[...] = jnp.zeros_like(dq_ref)
         stat_ref[...] = jnp.zeros_like(stat_ref)
+        each(n_past, wait_past)
 
     @pl.when(qstart < length)
     def _():
@@ -135,6 +202,7 @@
             return m_new, l * keep + fold(e, jnp.sum), d * keep + fold(e * dp, jnp.sum)
 
         def past_stats(b, carry, masked):
+            wait_past(b)
             r0 = pl.multiple_of(b * BK, BK)
             size = BK // 2
             parts = [pl.ds(r0 + k * size, size) for k in range(2)]
@@ -180,7 +248,7 @@
         full = offset // BK
         carry = lax.fori_loop(0, full, functools.partial(past_stats, masked=False), carry)
         m, l, d = lax.fori_loop(
-            full, (offset + BK - 1) // BK, functools.partial(past_stats, masked=True), carry
+            full, n_past, functools.partial(past_stats, masked=True), carry
         )
         l = jnp.sum(l, axis=0, keepdims=True)
         delta = jnp.sum(d, axis=0, keepdims=True) / l
@@ -228,17 +296,22 @@
         grid_spec=pltpu.PrefetchScalarGridSpec(
             num_scalar_prefetch=1,
             grid=(span // BQ,),
-            in_specs=[whole(a.shape) for a in (x, pk, pv)],
+            in_specs=[pl.BlockSpec(memory_space=pl.ANY)] * 3,
             out_specs=(
                 whole((n, 2, tok, DH)),
                 pl.BlockSpec((BQ, DH), lambda i, s: (i, 0)),
                 pl.BlockSpec((8, BQ), lambda i, s: (0, i)),
             ),
             scratch_shapes=[
+                pltpu.VMEM(x.shape, BF16),
+                pltpu.VMEM(pk.shape, BF16),
+                pltpu.VMEM(pv.shape, BF16),
                 pltpu.VMEM((span, BQ), F32),
                 pltpu.VMEM((span, BQ), F32),
                 pltpu.VMEM((span, DH), F32),
                 pltpu.VMEM((span, DH), F32),
+                pltpu.SemaphoreType.DMA((span // BQ,)),
+                pltpu.SemaphoreType.DMA((2, pk.shape[0] // BK)),
             ],
         ),
         compiler_params=pltpu.CompilerParams(vmem_limit_bytes=62 * MIB),

time: 165 us -> 164 us (level); the launches traced: 163 us -> 164 us
  Pallas kernels: 72.2 us -> 44.3 us
  starting transfers between devices: 33.2 us -> 53.1 us
  waiting for transfers between devices: 52.7 us -> 61.4 us
    ppermute x2, starting transfers between devices: 1.48 us -> 21.1 us  [from_behind(): lax.ppermute(block, axis, [((i - distance) % size, i) for i in range(size)])]
    pallas_call x2, Pallas kernels: 24.5 us -> 13.7 us  [past_grads(): pl.pallas_call(body, out_shape=jax.ShapeDtypeStruct(accum.shape, F32), gr...]
    all_to_all x3, waiting for transfers between devices: 48.8 us -> 59.6 us  [to_heads(): return lax.all_to_all(x, 'seq', split_axis=0, concat_axis=0, tiled=True)]
    pallas_call x1, Pallas kernels: 17.1 us -> 8.4 us  [query_grads(): pl.pallas_call(query_kernel, out_shape=jax.ShapeDtypeStruct((n, tok, DH),...]
    pallas_call x1, Pallas kernels: 24.9 us -> 17.8 us  [span_grads_and_stats(): pl.pallas_call(span_kernel, out_shape=(jax.ShapeDtypeStruct((n, 2, tok, D...]
    ppermute x2, waiting for transfers between devices: 3.86 us -> 1.75 us  [from_behind(): lax.ppermute(block, axis, [((i - distance) % size, i) for i in range(size)])]
  transfers between devices with their start and end apart: 5 -> 5, of which waited for: 3 -> 3; matrix products, arithmetic and copies ran while one was open for 1% -> 1% of each run, Pallas kernels for 26% -> 14%
where the time goes in v3:
time: 164 us
  waiting for transfers between devices  61.4 us (37%)
  starting transfers between devices  53.1 us (32%)
  Pallas kernels  44.3 us (27%)
  local copies, waits for them, and re-layouts  2.25 us (1%)
  between operations  1.99 us (1%)
    all_to_all x3, waiting for transfers between devices, to_heads(): return lax.all_to_all(x, 'seq', split_axis=0, concat_axis=0, tiled=True)  59.6 us
    all_to_all x3, starting transfers between devices, to_heads(): return lax.all_to_all(x, 'seq', split_axis=0, concat_axis=0, tiled=True)  32 us
    ppermute x2, starting transfers between devices, from_behind(): lax.ppermute(block, axis, [((i - distance) % size, i) for i in range(size)])  21.1 us
    pallas_call x1, Pallas kernels, span_grads_and_stats(): pl.pallas_call(span_kernel, out_shape=(jax.ShapeDtypeStruct((n, 2, tok, D...  17.8 us
    pallas_call x2, Pallas kernels, past_grads(): pl.pallas_call(body, out_shape=jax.ShapeDtypeStruct(accum.shape, F32), gr...  13.7 us
    pallas_call x1, Pallas kernels, query_grads(): pl.pallas_call(query_kernel, out_shape=jax.ShapeDtypeStruct((n, tok, DH),...  8.4 us
  transfers between devices with their start and end apart: 5, of which 3 were waited for; matrix products, arithmetic and copies ran while one was open for 1% of the time, Pallas kernels for 14%

profile of v3, /device:TPU:1, one launch (start us, length us, event | category | flops | bytes accessed | tf_op | source)
XLA Modules:
  0.0 163.6 jit_solution(13328542148552923601)
XLA Ops:
  0.6 2.6 %pack.1 = bf16[64,4,32,128]{3,2,1,0:T(8,128)(2,1)} custom-call(bf16[3,32,8192]{2,1,0:T(8,128)(2,1)} %bitcast.23, bf16[32,8192]{1,0:T(8,128)(2,1)} %bitcast.24), custom_call_target="tpu_custom_call" | custom-call | tf_op jit(solution)/shard_map/pack/pallas_call | solution.py:54
  3.2 0.0 copy-start
  3.2 13.3 %all-to-all-start = ((bf16[64,4,32,128]{3,2,1,0:T(8,128)(2,1)}), bf16[64,4,32,128]{3,2,1,0:T(8,128)(2,1)}, u32[]{:S(2)}, u32[]{:S(2)}) async-start(bf16[64,4,32,128]{3,2,1,0:T(8,128)(2,1)} %pack.1), calls=%async_computation | async-start | bytes 4194304 | tf_op jit(solution)/shard_map/all_to_all | solution.py:437
  17.8 0.0 copy-done
  17.8 0.2 copy.12
  18.1 0.6 pad_add_fusion.bounds.refs_0_
  18.6 1.3 slice_bitcast_fusion
  19.9 46.3 %all-to-all-done.x_hbm.x_ref.refs_1_ = bf16[64,4,32,128]{3,2,1,0:T(8,128)(2,1)} async-done(((bf16[64,4,32,128]{3,2,1,0:T(8,128)(2,1)}), bf16[64,4,32,128]{3,2,1,0:T(8,128)(2,1)}, u32[]{:S(2)}, u32[]{:S(2)}) %all-to-all-start) | async-done | bytes 2097184 | tf_op jit(solution)/shard_map/all_to_all | solution.py:437
  66.2 17.8 %attn_span.1 = (bf16[64,2,32,128]{3,2,1,0:T(8,128)(2,1)}, f32[2048,128]{1,0:T(8,128)}, f32[8,2048]{1,0:T(8,128)}) custom-call(s32[2]{0:T(128)} %pad_add_fusion.bounds.refs_0_, bf16[64,4,32,128]{3,2,1,0:T(8,128)(2,1)} %all-to-all-done.x_hbm.x_ref.refs_1_, bf16[3072,128]{1,0:T(8,128)(2,1)} %get-tuple-element.23.pk_hbm.pk_ref.refs_2_, ...), custom_call_target="tpu_custom_call" | custom-call | flops 7000000000 | bytes 6000000 | tf_op jit(solution)/shard_map/attn_span/pallas_call | solution.py:289
  84.0 7.2 %all-to-all-start.1 = ((bf16[64,2,32,128]{3,2,1,0:T(8,128)(2,1)}), bf16[64,2,32,128]{3,2,1,0:T(8,128)(2,1)}, u32[]{:S(2)}, u32[]{:S(2)}) async-start(bf16[64,2,32,128]{3,2,1,0:T(8,128)(2,1)} %get-tuple-element.11), calls=%async_computation.1 | async-start | bytes 2097152 | tf_op jit(solution)/shard_map/all_to_all | solution.py:437
  91.1 8.4 %attn_query.1 = bf16[64,32,128]{2,1,0:T(8,128)(2,1)} custom-call(s32[2]{0:T(128)} %pad_add_fusion.bounds.refs_0_, bf16[64,4,32,128]{3,2,1,0:T(8,128)(2,1)} %all-to-all-done.x_hbm.x_ref.refs_1_, bf16[3072,128]{1,0:T(8,128)(2,1)} %get-tuple-element.23.pk_hbm.pk_ref.refs_2_, bf16[3072,128]{1,0:T(8,128)(2,1)} %get-tuple-element.22.pv_hbm.pv_ref.refs_3_, ...), custom_call_target="tpu_custom_call" | custom-call | flops 5000000000 | bytes 6000000 | tf_op jit(solution)/shard_map/attn_query/pallas_call | solution.py:355
  99.6 17.8 %collective-permute-start = (bf16[64,32,128]{2,1,0:T(8,128)(2,1)}, bf16[64,32,128]{2,1,0:T(8,128)(2,1)S(1)}, u32[]{:S(2)}, u32[]{:S(2)}) collective-permute-start(bf16[64,32,128]{2,1,0:T(8,128)(2,1)} %attn_query.1), channel_id=1, source_target_pairs={{64,0},{128,64},{192,128},{0,192},{65,1},{129,65},{193,129},{1,193... | collective-permute-start | bytes 1572872 | tf_op jit(solution)/shard_map/ppermute | solution.py:442
  117.3 9.3 %attn_past0.1.prev_ref = f32[6144,128]{1,0:T(8,128)} custom-call(s32[2]{0:T(128)} %pad_add_fusion.bounds.refs_0_, bf16[64,4,32,128]{3,2,1,0:T(8,128)(2,1)} %all-to-all-done.x_hbm.x_ref.refs_1_, bf16[3072,128]{1,0:T(8,128)(2,1)} %get-tuple-element.23.pk_hbm.pk_ref.refs_2_, bf16[3072,128]{1,0:T(8,128)(2,1)} %get-tuple-element.22.pv_hbm.pv_ref.refs_3_, ...), custom_call_target="tpu_custom_call" | custom-call | flops 2000000000 | bytes 4000000 | tf_op jit(solution)/shard_map/attn_past0/pallas_call | solution.py:417
  126.6 1.7 %collective-permute-done = bf16[64,32,128]{2,1,0:T(8,128)(2,1)S(1)} collective-permute-done((bf16[64,32,128]{2,1,0:T(8,128)(2,1)}, bf16[64,32,128]{2,1,0:T(8,128)(2,1)S(1)}, u32[]{:S(2)}, u32[]{:S(2)}) %collective-permute-start) | collective-permute-done | bytes 524320 | tf_op jit(solution)/shard_map/ppermute | solution.py:442
  128.4 0.0 copy-start.1
  128.4 0.0 all-to-all-done.1
  128.4 0.8 copy-done.1
  129.2 3.3 %collective-permute-start.1 = (bf16[64,2,32,128]{3,2,1,0:T(8,128)(2,1)}, bf16[64,2,32,128]{3,2,1,0:T(8,128)(2,1)S(1)}, u32[]{:S(2)}, u32[]{:S(2)}) collective-permute-start(bf16[64,2,32,128]{3,2,1,0:T(8,128)(2,1)} %all-to-all-done.1), channel_id=1, source_target_pairs={{64,0},{128,64},{192,128},{0,192},{65,1},{129,65},{193,129},{1,193... | collective-permute-start | bytes 3145736 | tf_op jit(solution)/shard_map/ppermute | solution.py:442
  132.5 11.6 %all-to-all-start.2 = ((bf16[64,32,128]{2,1,0:T(8,128)(2,1)}), bf16[64,32,128]{2,1,0:T(8,128)(2,1)S(1)}, u32[]{:S(2)}, u32[]{:S(2)}) async-start(bf16[64,32,128]{2,1,0:T(8,128)(2,1)} %copy-done.1), calls=%async_computation.2 | async-start | bytes 1048576 | tf_op jit(solution)/shard_map/all_to_all | solution.py:437
  144.1 4.4 %attn_past1.1 = f32[6144,128]{1,0:T(8,128)} custom-call(s32[2]{0:T(128)} %pad_add_fusion.bounds.refs_0_, bf16[64,4,32,128]{3,2,1,0:T(8,128)(2,1)} %all-to-all-done.x_hbm.x_ref.refs_1_, bf16[3072,128]{1,0:T(8,128)(2,1)} %get-tuple-element.23.pk_hbm.pk_ref.refs_2_, ...), custom_call_target="tpu_custom_call", output_to_operand_aliasing={{}: (6, {})} | custom-call | flops 4000000000 | bytes 8000000 | tf_op jit(solution)/shard_map/attn_past1/pallas_call | solution.py:417
  148.4 13.3 %all-to-all-done.2.q_ref = bf16[64,32,128]{2,1,0:T(8,128)(2,1)S(1)} async-done(((bf16[64,32,128]{2,1,0:T(8,128)(2,1)}), bf16[64,32,128]{2,1,0:T(8,128)(2,1)S(1)}, u32[]{:S(2)}, u32[]{:S(2)}) %all-to-all-start.2) | async-done | bytes 524320 | tf_op jit(solution)/shard_map/all_to_all | solution.py:437
  161.8 0.0 collective-permute-done.1.kv_ref
  161.8 1.8 %unpack.1 = bf16[3,32,8192]{2,1,0:T(8,128)(2,1)} custom-call(bf16[64,32,128]{2,1,0:T(8,128)(2,1)S(1)} %all-to-all-done.2.q_ref, bf16[64,2,32,128]{3,2,1,0:T(8,128)(2,1)S(1)} %collective-permute-done.1.kv_ref), custom_call_target="tpu_custom_call" | custom-call | tf_op jit(solution)/shard_map/unpack/pallas_call | solution.py:81
Async XLA Ops:
  3.2 14.6 %copy-start = (bf16[1,3072,2,1,128]{4,2,3,1,0:T(2,128)(2,1)S(1)}, bf16[1,3072,2,1,128]{4,2,3,1,0:T(2,128)(2,1)}, u32[]{:S(2)}) copy-start(bf16[1,3072,2,1,128]{4,2,3,1,0:T(2,128)(2,1)} %param.8) | copy-start | bytes 4718596
  3.2 62.9 %all-to-all-start = ((bf16[64,4,32,128]{3,2,1,0:T(8,128)(2,1)}), bf16[64,4,32,128]{3,2,1,0:T(8,128)(2,1)}, u32[]{:S(2)}, u32[]{:S(2)}) async-start(bf16[64,4,32,128]{3,2,1,0:T(8,128)(2,1)} %pack.1), calls=%async_computation | async-start | bytes 4194304 | tf_op jit(solution)/shard_map/all_to_all | solution.py:437
  84.0 44.4 %all-to-all-start.1 = ((bf16[64,2,32,128]{3,2,1,0:T(8,128)(2,1)}), bf16[64,2,32,128]{3,2,1,0:T(8,128)(2,1)}, u32[]{:S(2)}, u32[]{:S(2)}) async-start(bf16[64,2,32,128]{3,2,1,0:T(8,128)(2,1)} %get-tuple-element.11), calls=%async_computation.1 | async-start | bytes 2097152 | tf_op jit(solution)/shard_map/all_to_all | solution.py:437
  99.6 28.8 %collective-permute-start = (bf16[64,32,128]{2,1,0:T(8,128)(2,1)}, bf16[64,32,128]{2,1,0:T(8,128)(2,1)S(1)}, u32[]{:S(2)}, u32[]{:S(2)}) collective-permute-start(bf16[64,32,128]{2,1,0:T(8,128)(2,1)} %attn_query.1), channel_id=1, source_target_pairs={{64,0},{128,64},{192,128},{0,192},{65,1},{129,65},{193,129},{1,193... | collective-permute-start | bytes 1572872 | tf_op jit(solution)/shard_map/ppermute | solution.py:442
  128.4 0.8 copy-start.1
  129.2 32.6 %collective-permute-start.1 = (bf16[64,2,32,128]{3,2,1,0:T(8,128)(2,1)}, bf16[64,2,32,128]{3,2,1,0:T(8,128)(2,1)S(1)}, u32[]{:S(2)}, u32[]{:S(2)}) collective-permute-start(bf16[64,2,32,128]{3,2,1,0:T(8,128)(2,1)} %all-to-all-done.1), channel_id=1, source_target_pairs={{64,0},{128,64},{192,128},{0,192},{65,1},{129,65},{193,129},{1,193... | collective-permute-start | bytes 3145736 | tf_op jit(solution)/shard_map/ppermute | solution.py:442
  132.5 29.3 %all-to-all-start.2 = ((bf16[64,32,128]{2,1,0:T(8,128)(2,1)}), bf16[64,32,128]{2,1,0:T(8,128)(2,1)S(1)}, u32[]{:S(2)}, u32[]{:S(2)}) async-start(bf16[64,32,128]{2,1,0:T(8,128)(2,1)} %copy-done.1), calls=%async_computation.2 | async-start | bytes 1048576 | tf_op jit(solution)/shard_map/all_to_all | solution.py:437

commit v4 on v3

--- a/solution.py
+++ b/solution.py
@@ -7,6 +7,7 @@
 from jax.experimental import pallas as pl
 from jax.experimental.pallas import tpu as pltpu
 from jax.sharding import PartitionSpec as P
+
 
 HEADS = 64
 DH = 128
@@ -320,24 +321,44 @@
     )(bounds, x, pk, pv)
 
 
-def query_kernel(bounds, x_ref, pk_ref, pv_ref, dqs_ref, stat_ref, o_ref):
-    tok = x_ref.shape[2]
+def query_kernel(
+    first, bounds, q_ref, g_ref, pk_hbm, pv_hbm, dqs_ref, stat_ref, o_ref, pk_ref, pv_ref, past_sem
+):
+    tok = q_ref.shape[2]
+    i = pl.program_id(0)
     offset = bounds[0]
     length = bounds[1]
-    qstart = pl.program_id(0) * BQ
+    qstart = (first + i) * BQ
+    n_past = (offset + BK - 1) // BK
+
+    def start_past(b):
+        for copy in past_copies(pk_hbm, pv_hbm, pk_ref, pv_ref, past_sem, b):
+            copy.start()
+
+    def wait_past(b):
+        @pl.when(i == 0)
+        def _():
+            for copy in past_copies(pk_hbm, pv_hbm, pk_ref, pv_ref, past_sem, b):
+                copy.wait()
+
+    @pl.when(i == 0)
+    def _():
+        each(n_past, start_past)
 
     @pl.when(qstart >= length)
     def _():
         o_ref[...] = jnp.zeros_like(o_ref)
+        each(n_past, wait_past)
 
     @pl.when(qstart < length)
     def _():
-        q_t = token_rows(x_ref, 0, qstart, BQ).T
-        g_t = live_rows(token_rows(x_ref, 3, qstart, BQ), qstart, length).T
+        q_t = q_ref[:, 0].reshape(BQ, DH).T
+        g_t = live_rows(g_ref[:, 0].reshape(BQ, DH), qstart, length).T
         lse = stat_ref[0:1]
         delta = stat_ref[1:2]
 
         def step(b, dq):
+            wait_past(b)
             r0 = pl.multiple_of(b * BK, BK)
             keys = pk_ref[pl.ds(r0, BK), :]
             p = jnp.exp2(mask_past(dot(keys, q_t), r0, offset) * SCALE_LOG2 - lse)
@@ -345,30 +366,40 @@
             ds = (p * (dp - delta)).astype(BF16)
             return dq + dot_rows(ds, keys)
 
-        dq = lax.fori_loop(0, (offset + BK - 1) // BK, step, dqs_ref[...])
+        dq = lax.fori_loop(0, n_past, step, dqs_ref[...])
         o_ref[...] = (dq * SCALE).astype(BF16).reshape(BQ // tok, tok, DH)
 
 
-def query_grads(bounds, x, pk, pv, dq_span, stats):
-    n, _, tok, _ = x.shape
-    span = n * tok
+def query_grads(bounds, x, pk, pv, dq_span, stats, first, count):
+    _, _, tok, _ = x.shape
+    group = BQ // tok
+    hbm = pl.BlockSpec(memory_space=pl.ANY)
     return pl.pallas_call(
-        query_kernel,
-        out_shape=jax.ShapeDtypeStruct((n, tok, DH), BF16),
+        functools.partial(query_kernel, first),
+        out_shape=jax.ShapeDtypeStruct((count * group, tok, DH), BF16),
         grid_spec=pltpu.PrefetchScalarGridSpec(
             num_scalar_prefetch=1,
-            grid=(span // BQ,),
-            in_specs=[whole(a.shape) for a in (x, pk, pv)]
-            + [
-                pl.BlockSpec((BQ, DH), lambda i, s: (i, 0)),
-                pl.BlockSpec((8, BQ), lambda i, s: (0, i)),
+            grid=(count,),
+            in_specs=[
+                pl.BlockSpec((group, 1, tok, DH), lambda i, s: (first + i, 0, 0, 0)),
+                pl.BlockSpec((group, 1, tok, DH), lambda i, s: (first + i, 3, 0, 0)),
+                hbm,
+                hbm,
+                pl.BlockSpec((BQ, DH), lambda i, s: (first + i, 0)),
+                pl.BlockSpec((8, BQ), lambda i, s: (0, first + i)),
             ],
-            out_specs=pl.BlockSpec((BQ // tok, tok, DH), lambda i, s: (i, 0, 0)),
+            out_specs=pl.BlockSpec((group, tok, DH), lambda i, s: (i, 0, 0)),
+            scratch_shapes=[
+                pltpu.VMEM(pk.shape, BF16),
+                pltpu.VMEM(pv.shape, BF16),
+                pltpu.SemaphoreType.DMA((2, pk.shape[0] // BK)),
+            ],
         ),
         compiler_params=pltpu.CompilerParams(vmem_limit_bytes=62 * MIB),
-        cost_estimate=pl.CostEstimate(flops=5 * 10**9, bytes_accessed=6 * 10**6, transcendentals=10**7),
-        name="attn_query",
-    )(bounds, x, pk, pv, dq_span, stats)
+        cost_estimate=pl.CostEstimate(
+            flops=10**9 * count, bytes_accessed=10**6 * count, transcendentals=2 * 10**6 * count
+        ),
+    )(bounds, x, x, pk, pv, dq_span, stats)
 
 
 def past_kernel(first, bounds, x_ref, pk_ref, pv_ref, stat_ref, acc_ref, prev_ref, nacc_ref, dk, dv):
@@ -429,7 +460,6 @@
         cost_estimate=pl.CostEstimate(
             flops=2 * 10**9 * count, bytes_accessed=4 * 10**6 * count, transcendentals=10**6 * count
         ),
-        name=f"attn_past{first}",
     )(*args)
 
 
@@ -450,12 +480,18 @@
     x = to_heads(pack(jnp.transpose(span_inputs[0], (1, 0, 2)), out_grad[0]))
     kv, dq_span, stats = span_grads_and_stats(bounds, x, pk, pv)
     kv = to_heads(kv)
-    dq = query_grads(bounds, x, pk, pv, dq_span, stats)
-    dq, bounds = lax.optimization_barrier((dq, bounds))
-    dq = from_behind(dq, "section", -1)
+    half = x.shape[0] * x.shape[2] // BQ // 2
+    low = query_grads(bounds, x, pk, pv, dq_span, stats, 0, half)
+    low, bounds = lax.optimization_barrier((low, bounds))
+    low = from_behind(low, "section", -1)
+    high = query_grads(bounds, x, pk, pv, dq_span, stats, half, half)
+    high, bounds = lax.optimization_barrier((high, bounds))
+    high = from_behind(high, "section", -1)
     accum = past_accum.reshape(past * 2, DH)
     new_accum = past_grads(bounds, x, pk, pv, stats, accum, 0, 1)
-    kv, dq, new_accum, bounds = lax.optimization_barrier((kv, dq, new_accum, bounds))
+    kv, dq, new_accum, bounds = lax.optimization_barrier(
+        (kv, jnp.concatenate([low, high]), new_accum, bounds)
+    )
     dq = to_heads(dq)
     kv = from_behind(kv, "section", -1)
     new_accum = past_grads(bounds, x, pk, pv, stats, accum, 1, past // BK - 1, new_accum)

time: 164 us -> 158 us (0.963)
  Pallas kernels: 44.3 us -> 59.5 us
  starting transfers between devices: 53.1 us -> 39.1 us
  waiting for transfers between devices: 61.4 us -> 53.4 us
    ppermute x2 -> x3, starting transfers between devices: 21.1 us -> 7.03 us  [from_behind(): lax.ppermute(block, axis, [((i - distance) % size, i) for i in range(size)])]
    pallas_call x1 -> x2, Pallas kernels: 8.4 us -> 17.4 us  [query_grads(): pl.pallas_call(functools.partial(query_kernel, first), out_shape=jax.Shap...]
    all_to_all x3, waiting for transfers between devices: 59.6 us -> 51.5 us  [to_heads(): return lax.all_to_all(x, 'seq', split_axis=0, concat_axis=0, tiled=True)]
    pallas_call x2, Pallas kernels: 13.7 us -> 20.6 us  [past_grads(): pl.pallas_call(body, out_shape=jax.ShapeDtypeStruct(accum.shape, F32), gr...]
  transfers between devices with their start and end apart: 5 -> 6, of which waited for: 3 -> 3; matrix products, arithmetic and copies ran while one was open for 1% -> 2% of each run, Pallas kernels for 14% -> 24%
where the time goes in v4:
time: 158 us; the launch traced here: 157 us
  Pallas kernels  59.5 us (38%)
  waiting for transfers between devices  53.4 us (34%)
  starting transfers between devices  39.1 us (25%)
  between operations  2.03 us (1%)
    all_to_all x3, waiting for transfers between devices, to_heads(): return lax.all_to_all(x, 'seq', split_axis=0, concat_axis=0, tiled=True)  51.5 us
    all_to_all x3, starting transfers between devices, to_heads(): return lax.all_to_all(x, 'seq', split_axis=0, concat_axis=0, tiled=True)  32 us
    pallas_call x2, Pallas kernels, past_grads(): pl.pallas_call(body, out_shape=jax.ShapeDtypeStruct(accum.shape, F32), gr...  20.6 us
    pallas_call x2, Pallas kernels, query_grads(): pl.pallas_call(functools.partial(query_kernel, first), out_shape=jax.Shap...  17.4 us
    pallas_call x1, Pallas kernels, span_grads_and_stats(): pl.pallas_call(span_kernel, out_shape=(jax.ShapeDtypeStruct((n, 2, tok, D...  17.1 us
    ppermute x3, starting transfers between devices, from_behind(): lax.ppermute(block, axis, [((i - distance) % size, i) for i in range(size)])  7.03 us
  transfers between devices with their start and end apart: 6, of which 3 were waited for; matrix products, arithmetic and copies ran while one was open for 2% of the time, Pallas kernels for 24%

profile of v4, /device:TPU:1, one launch (start us, length us, event | category | flops | bytes accessed | tf_op | source)
XLA Modules:
  0.0 157.0 jit_solution(3187267739199103296)
XLA Ops:
  0.6 2.6 %pack.1 = bf16[64,4,32,128]{3,2,1,0:T(8,128)(2,1)} custom-call(bf16[3,32,8192]{2,1,0:T(8,128)(2,1)} %bitcast.23, bf16[32,8192]{1,0:T(8,128)(2,1)} %bitcast.24), custom_call_target="tpu_custom_call" | custom-call | tf_op jit(solution)/shard_map/pack/pallas_call | solution.py:55
  3.2 0.0 copy-start
  3.2 13.3 %all-to-all-start = ((bf16[64,4,32,128]{3,2,1,0:T(8,128)(2,1)}), bf16[64,4,32,128]{3,2,1,0:T(8,128)(2,1)}, u32[]{:S(2)}, u32[]{:S(2)}) async-start(bf16[64,4,32,128]{3,2,1,0:T(8,128)(2,1)} %pack.1), calls=%async_computation | async-start | bytes 4194304 | tf_op jit(solution)/shard_map/all_to_all | solution.py:467
  17.8 0.0 copy-done
  17.8 0.2 copy.12
  18.1 0.7 pad_add_fusion.bounds.refs_0_
  18.7 1.2 slice_bitcast_fusion
  20.0 46.2 %all-to-all-done.x_hbm.q_ref.g_ref.refs_1_.x_ref = bf16[64,4,32,128]{3,2,1,0:T(8,128)(2,1)} async-done(((bf16[64,4,32,128]{3,2,1,0:T(8,128)(2,1)}), bf16[64,4,32,128]{3,2,1,0:T(8,128)(2,1)}, u32[]{:S(2)}, u32[]{:S(2)}) %all-to-all-start) | async-done | bytes 2097184 | tf_op jit(solution)/shard_map/all_to_all | solution.py:467
  66.2 17.1 %attn_span.1 = (bf16[64,2,32,128]{3,2,1,0:T(8,128)(2,1)}, f32[2048,128]{1,0:T(8,128)}, f32[8,2048]{1,0:T(8,128)}) custom-call(s32[2]{0:T(128)} %pad_add_fusion.bounds.refs_0_, bf16[64,4,32,128]{3,2,1,0:T(8,128)(2,1)} %all-to-all-done.x_hbm.q_ref.g_ref.refs_1_.x_ref, bf16[3072,128]{1,0:T(8,128)(2,1)} %get-tuple-element.27.pk_hbm.refs_2_.pk_ref, ...), custom_call_target="tpu_custom_call" | custom-call | flops 7000000000 | bytes 6000000 | tf_op jit(solution)/shard_map/attn_span/pallas_call | solution.py:290
  83.3 7.2 %all-to-all-start.1 = ((bf16[64,2,32,128]{3,2,1,0:T(8,128)(2,1)}), bf16[64,2,32,128]{3,2,1,0:T(8,128)(2,1)}, u32[]{:S(2)}, u32[]{:S(2)}) async-start(bf16[64,2,32,128]{3,2,1,0:T(8,128)(2,1)} %get-tuple-element.13), calls=%async_computation.1 | async-start | bytes 2097152 | tf_op jit(solution)/shard_map/all_to_all | solution.py:467
  90.5 10.3 %shard_map.77 = bf16[32,32,128]{2,1,0:T(8,128)(2,1)} custom-call(s32[2]{0:T(128)} %pad_add_fusion.bounds.refs_0_, bf16[64,4,32,128]{3,2,1,0:T(8,128)(2,1)} %all-to-all-done.x_hbm.q_ref.g_ref.refs_1_.x_ref, bf16[64,4,32,128]{3,2,1,0:T(8,128)(2,1)} %all-to-all-done.x_hbm.q_ref.g_ref.refs_1_.x_ref, bf16[3072,128]{1,0:T(8,128)(2,1)} %get-tuple-element.27.pk_hbm.refs_2_.pk_ref, ...), custom_call_target="tpu_custom_call" | custom-call | flops 2000000000 | bytes 2000000 | tf_op jit(solution)/shard_map/pallas_call | solution.py:377
  100.8 0.0 copy-start.1
  100.8 7.1 %shard_map.78 = bf16[32,32,128]{2,1,0:T(8,128)(2,1)} custom-call(s32[2]{0:T(128)} %pad_add_fusion.bounds.refs_0_, bf16[64,4,32,128]{3,2,1,0:T(8,128)(2,1)} %all-to-all-done.x_hbm.q_ref.g_ref.refs_1_.x_ref, bf16[64,4,32,128]{3,2,1,0:T(8,128)(2,1)} %all-to-all-done.x_hbm.q_ref.g_ref.refs_1_.x_ref, bf16[3072,128]{1,0:T(8,128)(2,1)} %get-tuple-element.27.pk_hbm.refs_2_.pk_ref, ...), custom_call_target="tpu_custom_call" | custom-call | flops 2000000000 | bytes 2000000 | tf_op jit(solution)/shard_map/pallas_call | solution.py:377
  108.0 0.1 collective-permute-start.1
  108.0 0.0 copy-done.1
  108.1 6.1 %collective-permute-start = (bf16[32,32,128]{2,1,0:T(8,128)(2,1)S(1)}, bf16[32,32,128]{2,1,0:T(8,128)(2,1)S(1)}, u32[]{:S(2)}, u32[]{:S(2)}) collective-permute-start(bf16[32,32,128]{2,1,0:T(8,128)(2,1)S(1)} %copy-done.1), channel_id=1, source_target_pairs={{64,0},{128,64},{192,128},{0,192},{65,1},{129,65},{193,129},{1,193... | collective-permute-start | bytes 786440 | tf_op jit(solution)/shard_map/ppermute | solution.py:472
  114.1 8.1 %shard_map.79.prev_ref = f32[6144,128]{1,0:T(8,128)} custom-call(s32[2]{0:T(128)} %pad_add_fusion.bounds.refs_0_, bf16[64,4,32,128]{3,2,1,0:T(8,128)(2,1)} %all-to-all-done.x_hbm.q_ref.g_ref.refs_1_.x_ref, bf16[3072,128]{1,0:T(8,128)(2,1)} %get-tuple-element.27.pk_hbm.refs_2_.pk_ref, bf16[3072,128]{1,0:T(8,128)(2,1)} %get-tuple-element.26.pv_hbm.refs_3_.pv_ref, ...), custom_call_target="tpu_custom_call" | custom-call | flops 2000000000 | bytes 4000000 | tf_op jit(solution)/shard_map/pallas_call | solution.py:448
  122.3 0.0 collective-permute-done.1
  122.3 1.9 %collective-permute-done = bf16[32,32,128]{2,1,0:T(8,128)(2,1)S(1)} collective-permute-done((bf16[32,32,128]{2,1,0:T(8,128)(2,1)S(1)}, bf16[32,32,128]{2,1,0:T(8,128)(2,1)S(1)}, u32[]{:S(2)}, u32[]{:S(2)}) %collective-permute-start) | collective-permute-done | bytes 262176 | tf_op jit(solution)/shard_map/ppermute | solution.py:472
  124.2 0.8 pad_maximum_fusion
  125.0 0.0 all-to-all-done.1
  125.0 0.9 collective-permute-start.2
  125.9 11.6 %all-to-all-start.2 = ((bf16[64,32,128]{2,1,0:T(8,128)(2,1)}), bf16[64,32,128]{2,1,0:T(8,128)(2,1)S(1)}, u32[]{:S(2)}, u32[]{:S(2)}) async-start(bf16[64,32,128]{2,1,0:T(8,128)(2,1)} %pad_maximum_fusion), calls=%async_computation.2 | async-start | bytes 1048576 | tf_op jit(solution)/shard_map/all_to_all | solution.py:467
  137.5 12.4 %shard_map.80 = f32[6144,128]{1,0:T(8,128)} custom-call(s32[2]{0:T(128)} %pad_add_fusion.bounds.refs_0_, bf16[64,4,32,128]{3,2,1,0:T(8,128)(2,1)} %all-to-all-done.x_hbm.q_ref.g_ref.refs_1_.x_ref, bf16[3072,128]{1,0:T(8,128)(2,1)} %get-tuple-element.27.pk_hbm.refs_2_.pk_ref, ...), custom_call_target="tpu_custom_call", output_to_operand_aliasing={{}: (6, {})} | custom-call | flops 4000000000 | bytes 8000000 | tf_op jit(solution)/shard_map/pallas_call | solution.py:448
  149.9 5.3 %all-to-all-done.2.q_ref = bf16[64,32,128]{2,1,0:T(8,128)(2,1)S(1)} async-done(((bf16[64,32,128]{2,1,0:T(8,128)(2,1)}), bf16[64,32,128]{2,1,0:T(8,128)(2,1)S(1)}, u32[]{:S(2)}, u32[]{:S(2)}) %all-to-all-start.2) | async-done | bytes 524320 | tf_op jit(solution)/shard_map/all_to_all | solution.py:467
  155.2 0.0 collective-permute-done.2.kv_ref
  155.2 1.8 %unpack.1 = bf16[3,32,8192]{2,1,0:T(8,128)(2,1)} custom-call(bf16[64,32,128]{2,1,0:T(8,128)(2,1)S(1)} %all-to-all-done.2.q_ref, bf16[64,2,32,128]{3,2,1,0:T(8,128)(2,1)S(1)} %collective-permute-done.2.kv_ref), custom_call_target="tpu_custom_call" | custom-call | tf_op jit(solution)/shard_map/unpack/pallas_call | solution.py:82
Async XLA Ops:
  3.2 14.6 %copy-start = (bf16[1,3072,2,1,128]{4,2,3,1,0:T(2,128)(2,1)S(1)}, bf16[1,3072,2,1,128]{4,2,3,1,0:T(2,128)(2,1)}, u32[]{:S(2)}) copy-start(bf16[1,3072,2,1,128]{4,2,3,1,0:T(2,128)(2,1)} %param.8) | copy-start | bytes 4718596
  3.2 62.9 %all-to-all-start = ((bf16[64,4,32,128]{3,2,1,0:T(8,128)(2,1)}), bf16[64,4,32,128]{3,2,1,0:T(8,128)(2,1)}, u32[]{:S(2)}, u32[]{:S(2)}) async-start(bf16[64,4,32,128]{3,2,1,0:T(8,128)(2,1)} %pack.1), calls=%async_computation | async-start | bytes 4194304 | tf_op jit(solution)/shard_map/all_to_all | solution.py:467
  83.3 41.7 %all-to-all-start.1 = ((bf16[64,2,32,128]{3,2,1,0:T(8,128)(2,1)}), bf16[64,2,32,128]{3,2,1,0:T(8,128)(2,1)}, u32[]{:S(2)}, u32[]{:S(2)}) async-start(bf16[64,2,32,128]{3,2,1,0:T(8,128)(2,1)} %get-tuple-element.13), calls=%async_computation.1 | async-start | bytes 2097152 | tf_op jit(solution)/shard_map/all_to_all | solution.py:467
  100.8 7.2 %copy-start.1 = (bf16[32,32,128]{2,1,0:T(8,128)(2,1)S(1)}, bf16[32,32,128]{2,1,0:T(8,128)(2,1)}, u32[]{:S(2)}) copy-start(bf16[32,32,128]{2,1,0:T(8,128)(2,1)} %shard_map.77) | copy-start | bytes 786436
  108.0 14.3 %collective-permute-start.1 = (bf16[32,32,128]{2,1,0:T(8,128)(2,1)}, bf16[32,32,128]{2,1,0:T(8,128)(2,1)S(1)}, u32[]{:S(2)}, u32[]{:S(2)}) collective-permute-start(bf16[32,32,128]{2,1,0:T(8,128)(2,1)} %shard_map.78), channel_id=1, source_target_pairs={{64,0},{128,64},{192,128},{0,192},{65,1},{129,65},{193,129},{1,193... | collective-permute-start | bytes 786440 | tf_op jit(solution)/shard_map/ppermute | solution.py:472
  108.1 16.1 %collective-permute-start = (bf16[32,32,128]{2,1,0:T(8,128)(2,1)S(1)}, bf16[32,32,128]{2,1,0:T(8,128)(2,1)S(1)}, u32[]{:S(2)}, u32[]{:S(2)}) collective-permute-start(bf16[32,32,128]{2,1,0:T(8,128)(2,1)S(1)} %copy-done.1), channel_id=1, source_target_pairs={{64,0},{128,64},{192,128},{0,192},{65,1},{129,65},{193,129},{1,193... | collective-permute-start | bytes 786440 | tf_op jit(solution)/shard_map/ppermute | solution.py:472
  125.0 30.2 %collective-permute-start.2 = (bf16[64,2,32,128]{3,2,1,0:T(8,128)(2,1)}, bf16[64,2,32,128]{3,2,1,0:T(8,128)(2,1)S(1)}, u32[]{:S(2)}, u32[]{:S(2)}) collective-permute-start(bf16[64,2,32,128]{3,2,1,0:T(8,128)(2,1)} %all-to-all-done.1), channel_id=1, source_target_pairs={{64,0},{128,64},{192,128},{0,192},{65,1},{129,65},{193,129},{1,193... | collective-permute-start | bytes 3145736 | tf_op jit(solution)/shard_map/ppermute | solution.py:472
  125.9 29.3 %all-to-all-start.2 = ((bf16[64,32,128]{2,1,0:T(8,128)(2,1)}), bf16[64,32,128]{2,1,0:T(8,128)(2,1)S(1)}, u32[]{:S(2)}, u32[]{:S(2)}) async-start(bf16[64,32,128]{2,1,0:T(8,128)(2,1)} %pad_maximum_fusion), calls=%async_computation.2 | async-start | bytes 1048576 | tf_op jit(solution)/shard_map/all_to_all | solution.py:467

commit v5 on v4

--- a/solution.py
+++ b/solution.py
@@ -69,32 +69,42 @@
     )(x, g)
 
 
-def unpack_kernel(q_ref, kv_ref, o_ref):
-    for h in range(q_ref.shape[0]):
-        cols = slice(h * DH, (h + 1) * DH)
-        o_ref[0, :, cols] = q_ref[h]
-        o_ref[1, :, cols] = kv_ref[h, 0]
-        o_ref[2, :, cols] = kv_ref[h, 1]
-
-
-def unpack(q, kv, heads_per_step=16):
-    rows = q.shape[1]
+def unpack_kernel(chunks, q_ref, kv_ref, o_hbm, o_ref, sem):
+    heads = HEADS // chunks
+    stores = []
+    for c in range(chunks):
+        for h in range(c * heads, (c + 1) * heads):
+            cols = slice(h * DH, (h + 1) * DH)
+            o_ref[0, :, cols] = q_ref[h]
+            o_ref[1, :, cols] = kv_ref[h, 0]
+            o_ref[2, :, cols] = kv_ref[h, 1]
+        cols = pl.ds(c * heads * DH, heads * DH)
+        stores.append(pltpu.make_async_copy(o_ref.at[:, :, cols], o_hbm.at[:, :, cols], sem.at[c]))
+        stores[-1].start()
+    for store in stores:
+        store.wait()
+
+
+def unpack(q, kv, chunks=8):
+    shape = (3, q.shape[1], HEADS * DH)
+    vmem = pl.BlockSpec(memory_space=pltpu.VMEM)
     return pl.pallas_call(
-        unpack_kernel,
-        out_shape=jax.ShapeDtypeStruct((3, rows, HEADS * DH), BF16),
-        grid=(HEADS // heads_per_step,),
-        in_specs=[
-            pl.BlockSpec((heads_per_step, rows, DH), lambda i: (i, 0, 0)),
-            pl.BlockSpec((heads_per_step, 2, rows, DH), lambda i: (i, 0, 0, 0)),
-        ],
-        out_specs=pl.BlockSpec((3, rows, heads_per_step * DH), lambda i: (0, 0, i)),
+        functools.partial(unpack_kernel, chunks),
+        out_shape=jax.ShapeDtypeStruct(shape, BF16),
+        in_specs=[vmem, vmem],
+        out_specs=pl.BlockSpec(memory_space=pl.ANY),
+        scratch_shapes=[pltpu.VMEM(shape, BF16), pltpu.SemaphoreType.DMA((chunks,))],
         compiler_params=pltpu.CompilerParams(vmem_limit_bytes=16 * MIB),
         name="unpack",
     )(q, kv)
 
 
 def whole(shape):
-    return pl.BlockSpec(shape, lambda i, s: (0,) * len(shape), pipeline_mode=pl.Buffered(1))
+    return pl.BlockSpec(shape, lambda i: (0,) * len(shape), pipeline_mode=pl.Buffered(1))
+
+
+def scalars():
+    return pl.BlockSpec(memory_space=pltpu.SMEM)
 
 
 def dot(a, b):
@@ -294,14 +304,13 @@
             jax.ShapeDtypeStruct((span, DH), F32),
             jax.ShapeDtypeStruct((8, span), F32),
         ),
-        grid_spec=pltpu.PrefetchScalarGridSpec(
-            num_scalar_prefetch=1,
+        grid_spec=pl.GridSpec(
             grid=(span // BQ,),
-            in_specs=[pl.BlockSpec(memory_space=pl.ANY)] * 3,
+            in_specs=[scalars()] + [pl.BlockSpec(memory_space=pl.ANY)] * 3,
             out_specs=(
                 whole((n, 2, tok, DH)),
-                pl.BlockSpec((BQ, DH), lambda i, s: (i, 0)),
-                pl.BlockSpec((8, BQ), lambda i, s: (0, i)),
+                pl.BlockSpec((BQ, DH), lambda i: (i, 0)),
+                pl.BlockSpec((8, BQ), lambda i: (0, i)),
             ),
             scratch_shapes=[
                 pltpu.VMEM(x.shape, BF16),
@@ -377,18 +386,18 @@
     return pl.pallas_call(
         functools.partial(query_kernel, first),
         out_shape=jax.ShapeDtypeStruct((count * group, tok, DH), BF16),
-        grid_spec=pltpu.PrefetchScalarGridSpec(
-            num_scalar_prefetch=1,
+        grid_spec=pl.GridSpec(
             grid=(count,),
             in_specs=[
-                pl.BlockSpec((group, 1, tok, DH), lambda i, s: (first + i, 0, 0, 0)),
-                pl.BlockSpec((group, 1, tok, DH), lambda i, s: (first + i, 3, 0, 0)),
+                scalars(),
+                pl.BlockSpec((group, 1, tok, DH), lambda i: (first + i, 0, 0, 0)),
+                pl.BlockSpec((group, 1, tok, DH), lambda i: (first + i, 3, 0, 0)),
                 hbm,
                 hbm,
-                pl.BlockSpec((BQ, DH), lambda i, s: (first + i, 0)),
-                pl.BlockSpec((8, BQ), lambda i, s: (0, first + i)),
+                pl.BlockSpec((BQ, DH), lambda i: (first + i, 0)),
+                pl.BlockSpec((8, BQ), lambda i: (0, first + i)),
             ],
-            out_specs=pl.BlockSpec((group, tok, DH), lambda i, s: (i, 0, 0)),
+            out_specs=pl.BlockSpec((group, tok, DH), lambda i: (i, 0, 0)),
             scratch_shapes=[
                 pltpu.VMEM(pk.shape, BF16),
                 pltpu.VMEM(pv.shape, BF16),
@@ -433,10 +442,10 @@
 
 
 def past_grads(bounds, x, pk, pv, stats, accum, first, count, prev=None):
-    keys = pl.BlockSpec((BK, DH), lambda i, s: (first + i, 0))
-    pairs = pl.BlockSpec((2 * BK, DH), lambda i, s: (first + i, 0))
+    keys = pl.BlockSpec((BK, DH), lambda i: (first + i, 0))
+    pairs = pl.BlockSpec((2 * BK, DH), lambda i: (first + i, 0))
     args = [bounds, x, pk, pv, stats, accum]
-    in_specs = [whole(x.shape), keys, keys, whole(stats.shape), pairs]
+    in_specs = [scalars(), whole(x.shape), keys, keys, whole(stats.shape), pairs]
     body = functools.partial(past_kernel, first)
     aliases = {}
     if prev is None:
@@ -448,8 +457,7 @@
     return pl.pallas_call(
         body,
         out_shape=jax.ShapeDtypeStruct(accum.shape, F32),
-        grid_spec=pltpu.PrefetchScalarGridSpec(
-            num_scalar_prefetch=1,
+        grid_spec=pl.GridSpec(
             grid=(count,),
             in_specs=in_specs,
             out_specs=pairs,

time: 158 us -> 156 us (0.987)
  Pallas kernels: 59.5 us -> 56.4 us
  transfers between devices with their start and end apart: 6 -> 6, of which waited for: 3 -> 3; matrix products, arithmetic and copies ran while one was open for 2% -> 2% of each run, Pallas kernels for 24% -> 23%
where the time goes in v5:
time: 156 us; the launch traced here: 155 us
  Pallas kernels  56.4 us (36%)
  waiting for transfers between devices  54.7 us (35%)
  starting transfers between devices  39 us (25%)
  between operations  2.19 us (1%)
    all_to_all x3, waiting for transfers between devices, to_heads(): return lax.all_to_all(x, 'seq', split_axis=0, concat_axis=0, tiled=True)  52.1 us
    all_to_all x3, starting transfers between devices, to_heads(): return lax.all_to_all(x, 'seq', split_axis=0, concat_axis=0, tiled=True)  32 us
    pallas_call x2, Pallas kernels, past_grads(): pl.pallas_call(body, out_shape=jax.ShapeDtypeStruct(accum.shape, F32), gr...  19.3 us
    pallas_call x1, Pallas kernels, span_grads_and_stats(): pl.pallas_call(span_kernel, out_shape=(jax.ShapeDtypeStruct((n, 2, tok, D...  17.2 us
    pallas_call x2, Pallas kernels, query_grads(): pl.pallas_call(functools.partial(query_kernel, first), out_shape=jax.Shap...  16.1 us
    ppermute x3, starting transfers between devices, from_behind(): lax.ppermute(block, axis, [((i - distance) % size, i) for i in range(size)])  7.02 us
  transfers between devices with their start and end apart: 6, of which 3 were waited for; matrix products, arithmetic and copies ran while one was open for 2% of the time, Pallas kernels for 23%

profile of v5, /device:TPU:1, one launch (start us, length us, event | category | flops | bytes accessed | tf_op | source)
XLA Modules:
  0.0 155.3 jit_solution(12092879598551122158)
XLA Ops:
  0.6 2.6 %pack.1 = bf16[64,4,32,128]{3,2,1,0:T(8,128)(2,1)} custom-call(bf16[3,32,8192]{2,1,0:T(8,128)(2,1)} %bitcast.23, bf16[32,8192]{1,0:T(8,128)(2,1)} %bitcast.24), custom_call_target="tpu_custom_call" | custom-call | tf_op jit(solution)/shard_map/pack/pallas_call | solution.py:55
  3.2 0.0 copy-start
  3.2 13.3 %all-to-all-start = ((bf16[64,4,32,128]{3,2,1,0:T(8,128)(2,1)}), bf16[64,4,32,128]{3,2,1,0:T(8,128)(2,1)}, u32[]{:S(2)}, u32[]{:S(2)}) async-start(bf16[64,4,32,128]{3,2,1,0:T(8,128)(2,1)} %pack.1), calls=%async_computation | async-start | bytes 4194304 | tf_op jit(solution)/shard_map/all_to_all | solution.py:475
  17.8 0.0 copy-done
  17.8 0.2 copy.12
  18.1 0.7 pad_add_fusion.bounds.refs_0_
  18.7 1.2 slice_bitcast_fusion
  20.0 46.2 %all-to-all-done.x_hbm.q_ref.g_ref.refs_1_.x_ref = bf16[64,4,32,128]{3,2,1,0:T(8,128)(2,1)} async-done(((bf16[64,4,32,128]{3,2,1,0:T(8,128)(2,1)}), bf16[64,4,32,128]{3,2,1,0:T(8,128)(2,1)}, u32[]{:S(2)}, u32[]{:S(2)}) %all-to-all-start) | async-done | bytes 2097184 | tf_op jit(solution)/shard_map/all_to_all | solution.py:475
  66.2 17.2 %attn_span.1 = (bf16[64,2,32,128]{3,2,1,0:T(8,128)(2,1)}, f32[2048,128]{1,0:T(8,128)}, f32[8,2048]{1,0:T(8,128)}) custom-call(s32[2]{0:T(128)} %pad_add_fusion.bounds.refs_0_, bf16[64,4,32,128]{3,2,1,0:T(8,128)(2,1)} %all-to-all-done.x_hbm.q_ref.g_ref.refs_1_.x_ref, bf16[3072,128]{1,0:T(8,128)(2,1)} %get-tuple-element.27.pk_hbm.refs_2_.pk_ref, ...), custom_call_target="tpu_custom_call" | custom-call | flops 7000000000 | bytes 6000000 | tf_op jit(solution)/shard_map/attn_span/pallas_call | solution.py:300
  83.3 7.2 %all-to-all-start.1 = ((bf16[64,2,32,128]{3,2,1,0:T(8,128)(2,1)}), bf16[64,2,32,128]{3,2,1,0:T(8,128)(2,1)}, u32[]{:S(2)}, u32[]{:S(2)}) async-start(bf16[64,2,32,128]{3,2,1,0:T(8,128)(2,1)} %get-tuple-element.13), calls=%async_computation.1 | async-start | bytes 2097152 | tf_op jit(solution)/shard_map/all_to_all | solution.py:475
  90.5 9.7 %shard_map.77 = bf16[32,32,128]{2,1,0:T(8,128)(2,1)} custom-call(s32[2]{0:T(128)} %pad_add_fusion.bounds.refs_0_, bf16[64,4,32,128]{3,2,1,0:T(8,128)(2,1)} %all-to-all-done.x_hbm.q_ref.g_ref.refs_1_.x_ref, bf16[64,4,32,128]{3,2,1,0:T(8,128)(2,1)} %all-to-all-done.x_hbm.q_ref.g_ref.refs_1_.x_ref, bf16[3072,128]{1,0:T(8,128)(2,1)} %get-tuple-element.27.pk_hbm.refs_2_.pk_ref, ...), custom_call_target="tpu_custom_call" | custom-call | flops 2000000000 | bytes 2000000 | tf_op jit(solution)/shard_map/pallas_call | solution.py:386
  100.2 0.0 copy-start.1
  100.2 6.4 %shard_map.78 = bf16[32,32,128]{2,1,0:T(8,128)(2,1)} custom-call(s32[2]{0:T(128)} %pad_add_fusion.bounds.refs_0_, bf16[64,4,32,128]{3,2,1,0:T(8,128)(2,1)} %all-to-all-done.x_hbm.q_ref.g_ref.refs_1_.x_ref, bf16[64,4,32,128]{3,2,1,0:T(8,128)(2,1)} %all-to-all-done.x_hbm.q_ref.g_ref.refs_1_.x_ref, bf16[3072,128]{1,0:T(8,128)(2,1)} %get-tuple-element.27.pk_hbm.refs_2_.pk_ref, ...), custom_call_target="tpu_custom_call" | custom-call | flops 2000000000 | bytes 2000000 | tf_op jit(solution)/shard_map/pallas_call | solution.py:386
  106.6 0.1 collective-permute-start.1
  106.7 0.0 copy-done.1
  106.7 6.1 %collective-permute-start = (bf16[32,32,128]{2,1,0:T(8,128)(2,1)S(1)}, bf16[32,32,128]{2,1,0:T(8,128)(2,1)S(1)}, u32[]{:S(2)}, u32[]{:S(2)}) collective-permute-start(bf16[32,32,128]{2,1,0:T(8,128)(2,1)S(1)} %copy-done.1), channel_id=1, source_target_pairs={{64,0},{128,64},{192,128},{0,192},{65,1},{129,65},{193,129},{1,193... | collective-permute-start | bytes 786440 | tf_op jit(solution)/shard_map/ppermute | solution.py:480
  112.8 7.5 %shard_map.79.prev_ref = f32[6144,128]{1,0:T(8,128)} custom-call(s32[2]{0:T(128)} %pad_add_fusion.bounds.refs_0_, bf16[64,4,32,128]{3,2,1,0:T(8,128)(2,1)} %all-to-all-done.x_hbm.q_ref.g_ref.refs_1_.x_ref, bf16[3072,128]{1,0:T(8,128)(2,1)} %get-tuple-element.27.pk_hbm.refs_2_.pk_ref, bf16[3072,128]{1,0:T(8,128)(2,1)} %get-tuple-element.26.pv_hbm.refs_3_.pv_ref, ...), custom_call_target="tpu_custom_call" | custom-call | flops 2000000000 | bytes 4000000 | tf_op jit(solution)/shard_map/pallas_call | solution.py:457
  120.3 0.0 collective-permute-done.1
  120.3 2.6 %collective-permute-done = bf16[32,32,128]{2,1,0:T(8,128)(2,1)S(1)} collective-permute-done((bf16[32,32,128]{2,1,0:T(8,128)(2,1)S(1)}, bf16[32,32,128]{2,1,0:T(8,128)(2,1)S(1)}, u32[]{:S(2)}, u32[]{:S(2)}) %collective-permute-start) | collective-permute-done | bytes 262176 | tf_op jit(solution)/shard_map/ppermute | solution.py:480
  122.9 0.8 pad_maximum_fusion
  123.7 0.0 all-to-all-done.1
  123.7 0.9 collective-permute-start.2
  124.6 11.6 %all-to-all-start.2 = ((bf16[64,32,128]{2,1,0:T(8,128)(2,1)}), bf16[64,32,128]{2,1,0:T(8,128)(2,1)S(1)}, u32[]{:S(2)}, u32[]{:S(2)}) async-start(bf16[64,32,128]{2,1,0:T(8,128)(2,1)} %pad_maximum_fusion), calls=%async_computation.2 | async-start | bytes 1048576 | tf_op jit(solution)/shard_map/all_to_all | solution.py:475
  136.2 11.8 %shard_map.80 = f32[6144,128]{1,0:T(8,128)} custom-call(s32[2]{0:T(128)} %pad_add_fusion.bounds.refs_0_, bf16[64,4,32,128]{3,2,1,0:T(8,128)(2,1)} %all-to-all-done.x_hbm.q_ref.g_ref.refs_1_.x_ref, bf16[3072,128]{1,0:T(8,128)(2,1)} %get-tuple-element.27.pk_hbm.refs_2_.pk_ref, ...), custom_call_target="tpu_custom_call", output_to_operand_aliasing={{}: (6, {})} | custom-call | flops 4000000000 | bytes 8000000 | tf_op jit(solution)/shard_map/pallas_call | solution.py:457
  148.0 5.9 %all-to-all-done.2.q_ref = bf16[64,32,128]{2,1,0:T(8,128)(2,1)S(1)} async-done(((bf16[64,32,128]{2,1,0:T(8,128)(2,1)}), bf16[64,32,128]{2,1,0:T(8,128)(2,1)S(1)}, u32[]{:S(2)}, u32[]{:S(2)}) %all-to-all-start.2) | async-done | bytes 524320 | tf_op jit(solution)/shard_map/all_to_all | solution.py:475
  153.9 0.0 collective-permute-done.2.kv_ref
  153.9 1.2 unpack.1
Async XLA Ops:
  3.2 14.6 %copy-start = (bf16[1,3072,2,1,128]{4,2,3,1,0:T(2,128)(2,1)S(1)}, bf16[1,3072,2,1,128]{4,2,3,1,0:T(2,128)(2,1)}, u32[]{:S(2)}) copy-start(bf16[1,3072,2,1,128]{4,2,3,1,0:T(2,128)(2,1)} %param.8) | copy-start | bytes 4718596
  3.2 62.9 %all-to-all-start = ((bf16[64,4,32,128]{3,2,1,0:T(8,128)(2,1)}), bf16[64,4,32,128]{3,2,1,0:T(8,128)(2,1)}, u32[]{:S(2)}, u32[]{:S(2)}) async-start(bf16[64,4,32,128]{3,2,1,0:T(8,128)(2,1)} %pack.1), calls=%async_computation | async-start | bytes 4194304 | tf_op jit(solution)/shard_map/all_to_all | solution.py:475
  83.3 40.4 %all-to-all-start.1 = ((bf16[64,2,32,128]{3,2,1,0:T(8,128)(2,1)}), bf16[64,2,32,128]{3,2,1,0:T(8,128)(2,1)}, u32[]{:S(2)}, u32[]{:S(2)}) async-start(bf16[64,2,32,128]{3,2,1,0:T(8,128)(2,1)} %get-tuple-element.13), calls=%async_computation.1 | async-start | bytes 2097152 | tf_op jit(solution)/shard_map/all_to_all | solution.py:475
  100.2 6.5 %copy-start.1 = (bf16[32,32,128]{2,1,0:T(8,128)(2,1)S(1)}, bf16[32,32,128]{2,1,0:T(8,128)(2,1)}, u32[]{:S(2)}) copy-start(bf16[32,32,128]{2,1,0:T(8,128)(2,1)} %shard_map.77) | copy-start | bytes 786436
  106.6 13.7 %collective-permute-start.1 = (bf16[32,32,128]{2,1,0:T(8,128)(2,1)}, bf16[32,32,128]{2,1,0:T(8,128)(2,1)S(1)}, u32[]{:S(2)}, u32[]{:S(2)}) collective-permute-start(bf16[32,32,128]{2,1,0:T(8,128)(2,1)} %shard_map.78), channel_id=1, source_target_pairs={{64,0},{128,64},{192,128},{0,192},{65,1},{129,65},{193,129},{1,193... | collective-permute-start | bytes 786440 | tf_op jit(solution)/shard_map/ppermute | solution.py:480
  106.7 16.2 %collective-permute-start = (bf16[32,32,128]{2,1,0:T(8,128)(2,1)S(1)}, bf16[32,32,128]{2,1,0:T(8,128)(2,1)S(1)}, u32[]{:S(2)}, u32[]{:S(2)}) collective-permute-start(bf16[32,32,128]{2,1,0:T(8,128)(2,1)S(1)} %copy-done.1), channel_id=1, source_target_pairs={{64,0},{128,64},{192,128},{0,192},{65,1},{129,65},{193,129},{1,193... | collective-permute-start | bytes 786440 | tf_op jit(solution)/shard_map/ppermute | solution.py:480
  123.7 30.1 %collective-permute-start.2 = (bf16[64,2,32,128]{3,2,1,0:T(8,128)(2,1)}, bf16[64,2,32,128]{3,2,1,0:T(8,128)(2,1)S(1)}, u32[]{:S(2)}, u32[]{:S(2)}) collective-permute-start(bf16[64,2,32,128]{3,2,1,0:T(8,128)(2,1)} %all-to-all-done.1), channel_id=1, source_target_pairs={{64,0},{128,64},{192,128},{0,192},{65,1},{129,65},{193,129},{1,193... | collective-permute-start | bytes 3145736 | tf_op jit(solution)/shard_map/ppermute | solution.py:480
  124.6 29.3 %all-to-all-start.2 = ((bf16[64,32,128]{2,1,0:T(8,128)(2,1)}), bf16[64,32,128]{2,1,0:T(8,128)(2,1)S(1)}, u32[]{:S(2)}, u32[]{:S(2)}) async-start(bf16[64,32,128]{2,1,0:T(8,128)(2,1)} %pad_maximum_fusion), calls=%async_computation.2 | async-start | bytes 1048576 | tf_op jit(solution)/shard_map/all_to_all | solution.py:475

commit v6 on v5

--- a/solution.py
+++ b/solution.py
@@ -18,6 +18,7 @@
 BF16 = jnp.bfloat16
 BQ = 512
 BK = 1024
+PK = 768
 MIB = 2**20
 
 
@@ -415,7 +416,7 @@
     del prev_ref
     offset = bounds[0]
     length = bounds[1]
-    kstart = (first + pl.program_id(0)) * BK
+    kstart = (first + pl.program_id(0)) * PK
     dk[...] = jnp.zeros_like(dk)
     dv[...] = jnp.zeros_like(dv)
 
@@ -435,15 +436,15 @@
     def _():
         lax.fori_loop(0, (length + BQ - 1) // BQ, step, 0)
 
-    even = pl.ds(0, BK, stride=2)
-    odd = pl.ds(1, BK, stride=2)
+    even = pl.ds(0, PK, stride=2)
+    odd = pl.ds(1, PK, stride=2)
     nacc_ref[even, :] = acc_ref[even, :] + dk[...] * SCALE
     nacc_ref[odd, :] = acc_ref[odd, :] + dv[...]
 
 
 def past_grads(bounds, x, pk, pv, stats, accum, first, count, prev=None):
-    keys = pl.BlockSpec((BK, DH), lambda i: (first + i, 0))
-    pairs = pl.BlockSpec((2 * BK, DH), lambda i: (first + i, 0))
+    keys = pl.BlockSpec((PK, DH), lambda i: (first + i, 0))
+    pairs = pl.BlockSpec((2 * PK, DH), lambda i: (first + i, 0))
     args = [bounds, x, pk, pv, stats, accum]
     in_specs = [scalars(), whole(x.shape), keys, keys, whole(stats.shape), pairs]
     body = functools.partial(past_kernel, first)
@@ -461,7 +462,7 @@
             grid=(count,),
             in_specs=in_specs,
             out_specs=pairs,
-            scratch_shapes=[pltpu.VMEM((BK, DH), F32), pltpu.VMEM((BK, DH), F32)],
+            scratch_shapes=[pltpu.VMEM((PK, DH), F32), pltpu.VMEM((PK, DH), F32)],
         ),
         input_output_aliases=aliases,
         compiler_params=pltpu.CompilerParams(vmem_limit_bytes=62 * MIB),
@@ -502,7 +503,7 @@
     )
     dq = to_heads(dq)
     kv = from_behind(kv, "section", -1)
-    new_accum = past_grads(bounds, x, pk, pv, stats, accum, 1, past // BK - 1, new_accum)
+    new_accum = past_grads(bounds, x, pk, pv, stats, accum, 1, past // PK - 1, new_accum)
     out = jnp.transpose(unpack(dq, kv), (1, 0, 2))
     return out[None], new_accum.reshape(past_accum.shape)
 

time: 156 us -> 156 us (level)
  no operation moved by 1% of the time
where the time goes in v6:
time: 156 us; the launch traced here: 155 us
  Pallas kernels  56.5 us (36%)
  waiting for transfers between devices  54.6 us (35%)
  starting transfers between devices  39 us (25%)
  between operations  2.19 us (1%)
    all_to_all x3, waiting for transfers between devices, to_heads(): return lax.all_to_all(x, 'seq', split_axis=0, concat_axis=0, tiled=True)  50.8 us
    all_to_all x3, starting transfers between devices, to_heads(): return lax.all_to_all(x, 'seq', split_axis=0, concat_axis=0, tiled=True)  32 us
    pallas_call x2, Pallas kernels, past_grads(): pl.pallas_call(body, out_shape=jax.ShapeDtypeStruct(accum.shape, F32), gr...  19.4 us
    pallas_call x1, Pallas kernels, span_grads_and_stats(): pl.pallas_call(span_kernel, out_shape=(jax.ShapeDtypeStruct((n, 2, tok, D...  17.2 us
    pallas_call x2, Pallas kernels, query_grads(): pl.pallas_call(functools.partial(query_kernel, first), out_shape=jax.Shap...  16.1 us
    ppermute x3, starting transfers between devices, from_behind(): lax.ppermute(block, axis, [((i - distance) % size, i) for i in range(size)])  7.02 us
    ppermute x3, waiting for transfers between devices, from_behind(): lax.ppermute(block, axis, [((i - distance) % size, i) for i in range(size)])  3.78 us
  transfers between devices with their start and end apart: 6, of which 3 were waited for; matrix products, arithmetic and copies ran while one was open for 2% of the time, Pallas kernels for 23%

profile of v6, /device:TPU:1, one launch (start us, length us, event | category | flops | bytes accessed | tf_op | source)
XLA Modules:
  0.0 155.3 jit_solution(14246779041900518837)
XLA Ops:
  0.6 2.6 %pack.1 = bf16[64,4,32,128]{3,2,1,0:T(8,128)(2,1)} custom-call(bf16[3,32,8192]{2,1,0:T(8,128)(2,1)} %bitcast.23, bf16[32,8192]{1,0:T(8,128)(2,1)} %bitcast.24), custom_call_target="tpu_custom_call" | custom-call | tf_op jit(solution)/shard_map/pack/pallas_call | solution.py:56
  3.2 0.0 copy-start
  3.2 13.3 %all-to-all-start = ((bf16[64,4,32,128]{3,2,1,0:T(8,128)(2,1)}), bf16[64,4,32,128]{3,2,1,0:T(8,128)(2,1)}, u32[]{:S(2)}, u32[]{:S(2)}) async-start(bf16[64,4,32,128]{3,2,1,0:T(8,128)(2,1)} %pack.1), calls=%async_computation | async-start | bytes 4194304 | tf_op jit(solution)/shard_map/all_to_all | solution.py:476
  17.8 0.0 copy-done
  17.8 0.2 copy.12
  18.1 0.7 pad_add_fusion.bounds.refs_0_
  18.7 1.2 slice_bitcast_fusion
  20.0 46.2 %all-to-all-done.x_hbm.q_ref.g_ref.refs_1_.x_ref = bf16[64,4,32,128]{3,2,1,0:T(8,128)(2,1)} async-done(((bf16[64,4,32,128]{3,2,1,0:T(8,128)(2,1)}), bf16[64,4,32,128]{3,2,1,0:T(8,128)(2,1)}, u32[]{:S(2)}, u32[]{:S(2)}) %all-to-all-start) | async-done | bytes 2097184 | tf_op jit(solution)/shard_map/all_to_all | solution.py:476
  66.2 17.2 %attn_span.1 = (bf16[64,2,32,128]{3,2,1,0:T(8,128)(2,1)}, f32[2048,128]{1,0:T(8,128)}, f32[8,2048]{1,0:T(8,128)}) custom-call(s32[2]{0:T(128)} %pad_add_fusion.bounds.refs_0_, bf16[64,4,32,128]{3,2,1,0:T(8,128)(2,1)} %all-to-all-done.x_hbm.q_ref.g_ref.refs_1_.x_ref, bf16[3072,128]{1,0:T(8,128)(2,1)} %get-tuple-element.27.pk_hbm.refs_2_.pk_ref, ...), custom_call_target="tpu_custom_call" | custom-call | flops 7000000000 | bytes 6000000 | tf_op jit(solution)/shard_map/attn_span/pallas_call | solution.py:301
  83.3 7.2 %all-to-all-start.1 = ((bf16[64,2,32,128]{3,2,1,0:T(8,128)(2,1)}), bf16[64,2,32,128]{3,2,1,0:T(8,128)(2,1)}, u32[]{:S(2)}, u32[]{:S(2)}) async-start(bf16[64,2,32,128]{3,2,1,0:T(8,128)(2,1)} %get-tuple-element.13), calls=%async_computation.1 | async-start | bytes 2097152 | tf_op jit(solution)/shard_map/all_to_all | solution.py:476
  90.5 9.7 %shard_map.77 = bf16[32,32,128]{2,1,0:T(8,128)(2,1)} custom-call(s32[2]{0:T(128)} %pad_add_fusion.bounds.refs_0_, bf16[64,4,32,128]{3,2,1,0:T(8,128)(2,1)} %all-to-all-done.x_hbm.q_ref.g_ref.refs_1_.x_ref, bf16[64,4,32,128]{3,2,1,0:T(8,128)(2,1)} %all-to-all-done.x_hbm.q_ref.g_ref.refs_1_.x_ref, bf16[3072,128]{1,0:T(8,128)(2,1)} %get-tuple-element.27.pk_hbm.refs_2_.pk_ref, ...), custom_call_target="tpu_custom_call" | custom-call | flops 2000000000 | bytes 2000000 | tf_op jit(solution)/shard_map/pallas_call | solution.py:387
  100.2 0.0 copy-start.1
  100.2 6.4 %shard_map.78 = bf16[32,32,128]{2,1,0:T(8,128)(2,1)} custom-call(s32[2]{0:T(128)} %pad_add_fusion.bounds.refs_0_, bf16[64,4,32,128]{3,2,1,0:T(8,128)(2,1)} %all-to-all-done.x_hbm.q_ref.g_ref.refs_1_.x_ref, bf16[64,4,32,128]{3,2,1,0:T(8,128)(2,1)} %all-to-all-done.x_hbm.q_ref.g_ref.refs_1_.x_ref, bf16[3072,128]{1,0:T(8,128)(2,1)} %get-tuple-element.27.pk_hbm.refs_2_.pk_ref, ...), custom_call_target="tpu_custom_call" | custom-call | flops 2000000000 | bytes 2000000 | tf_op jit(solution)/shard_map/pallas_call | solution.py:387
  106.6 0.1 collective-permute-start.1
  106.7 0.0 copy-done.1
  106.7 6.1 %collective-permute-start = (bf16[32,32,128]{2,1,0:T(8,128)(2,1)S(1)}, bf16[32,32,128]{2,1,0:T(8,128)(2,1)S(1)}, u32[]{:S(2)}, u32[]{:S(2)}) collective-permute-start(bf16[32,32,128]{2,1,0:T(8,128)(2,1)S(1)} %copy-done.1), channel_id=1, source_target_pairs={{64,0},{128,64},{192,128},{0,192},{65,1},{129,65},{193,129},{1,193... | collective-permute-start | bytes 786440 | tf_op jit(solution)/shard_map/ppermute | solution.py:481
  112.8 6.3 %shard_map.79.prev_ref = f32[6144,128]{1,0:T(8,128)} custom-call(s32[2]{0:T(128)} %pad_add_fusion.bounds.refs_0_, bf16[64,4,32,128]{3,2,1,0:T(8,128)(2,1)} %all-to-all-done.x_hbm.q_ref.g_ref.refs_1_.x_ref, bf16[3072,128]{1,0:T(8,128)(2,1)} %get-tuple-element.27.pk_hbm.refs_2_.pk_ref, bf16[3072,128]{1,0:T(8,128)(2,1)} %get-tuple-element.26.pv_hbm.refs_3_.pv_ref, ...), custom_call_target="tpu_custom_call" | custom-call | flops 2000000000 | bytes 4000000 | tf_op jit(solution)/shard_map/pallas_call | solution.py:458
  119.1 0.0 collective-permute-done.1
  119.1 3.8 %collective-permute-done = bf16[32,32,128]{2,1,0:T(8,128)(2,1)S(1)} collective-permute-done((bf16[32,32,128]{2,1,0:T(8,128)(2,1)S(1)}, bf16[32,32,128]{2,1,0:T(8,128)(2,1)S(1)}, u32[]{:S(2)}, u32[]{:S(2)}) %collective-permute-start) | collective-permute-done | bytes 262176 | tf_op jit(solution)/shard_map/ppermute | solution.py:481
  122.9 0.8 pad_maximum_fusion
  123.7 0.0 all-to-all-done.1
  123.7 0.9 collective-permute-start.2
  124.6 11.6 %all-to-all-start.2 = ((bf16[64,32,128]{2,1,0:T(8,128)(2,1)}), bf16[64,32,128]{2,1,0:T(8,128)(2,1)S(1)}, u32[]{:S(2)}, u32[]{:S(2)}) async-start(bf16[64,32,128]{2,1,0:T(8,128)(2,1)} %pad_maximum_fusion), calls=%async_computation.2 | async-start | bytes 1048576 | tf_op jit(solution)/shard_map/all_to_all | solution.py:476
  136.2 13.1 %shard_map.80 = f32[6144,128]{1,0:T(8,128)} custom-call(s32[2]{0:T(128)} %pad_add_fusion.bounds.refs_0_, bf16[64,4,32,128]{3,2,1,0:T(8,128)(2,1)} %all-to-all-done.x_hbm.q_ref.g_ref.refs_1_.x_ref, bf16[3072,128]{1,0:T(8,128)(2,1)} %get-tuple-element.27.pk_hbm.refs_2_.pk_ref, ...), custom_call_target="tpu_custom_call", output_to_operand_aliasing={{}: (6, {})} | custom-call | flops 6000000000 | bytes 12000000 | tf_op jit(solution)/shard_map/pallas_call | solution.py:458
  149.2 4.6 %all-to-all-done.2.q_ref = bf16[64,32,128]{2,1,0:T(8,128)(2,1)S(1)} async-done(((bf16[64,32,128]{2,1,0:T(8,128)(2,1)}), bf16[64,32,128]{2,1,0:T(8,128)(2,1)S(1)}, u32[]{:S(2)}, u32[]{:S(2)}) %all-to-all-start.2) | async-done | bytes 524320 | tf_op jit(solution)/shard_map/all_to_all | solution.py:476
  153.9 0.0 collective-permute-done.2.kv_ref
  153.9 1.2 unpack.1
Async XLA Ops:
  3.2 14.6 %copy-start = (bf16[1,3072,2,1,128]{4,2,3,1,0:T(2,128)(2,1)S(1)}, bf16[1,3072,2,1,128]{4,2,3,1,0:T(2,128)(2,1)}, u32[]{:S(2)}) copy-start(bf16[1,3072,2,1,128]{4,2,3,1,0:T(2,128)(2,1)} %param.8) | copy-start | bytes 4718596
  3.2 62.9 %all-to-all-start = ((bf16[64,4,32,128]{3,2,1,0:T(8,128)(2,1)}), bf16[64,4,32,128]{3,2,1,0:T(8,128)(2,1)}, u32[]{:S(2)}, u32[]{:S(2)}) async-start(bf16[64,4,32,128]{3,2,1,0:T(8,128)(2,1)} %pack.1), calls=%async_computation | async-start | bytes 4194304 | tf_op jit(solution)/shard_map/all_to_all | solution.py:476
  83.3 40.4 %all-to-all-start.1 = ((bf16[64,2,32,128]{3,2,1,0:T(8,128)(2,1)}), bf16[64,2,32,128]{3,2,1,0:T(8,128)(2,1)}, u32[]{:S(2)}, u32[]{:S(2)}) async-start(bf16[64,2,32,128]{3,2,1,0:T(8,128)(2,1)} %get-tuple-element.13), calls=%async_computation.1 | async-start | bytes 2097152 | tf_op jit(solution)/shard_map/all_to_all | solution.py:476
  100.2 6.5 %copy-start.1 = (bf16[32,32,128]{2,1,0:T(8,128)(2,1)S(1)}, bf16[32,32,128]{2,1,0:T(8,128)(2,1)}, u32[]{:S(2)}) copy-start(bf16[32,32,128]{2,1,0:T(8,128)(2,1)} %shard_map.77) | copy-start | bytes 786436
  106.6 12.5 %collective-permute-start.1 = (bf16[32,32,128]{2,1,0:T(8,128)(2,1)}, bf16[32,32,128]{2,1,0:T(8,128)(2,1)S(1)}, u32[]{:S(2)}, u32[]{:S(2)}) collective-permute-start(bf16[32,32,128]{2,1,0:T(8,128)(2,1)} %shard_map.78), channel_id=1, source_target_pairs={{64,0},{128,64},{192,128},{0,192},{65,1},{129,65},{193,129},{1,193... | collective-permute-start | bytes 786440 | tf_op jit(solution)/shard_map/ppermute | solution.py:481
  106.7 16.2 %collective-permute-start = (bf16[32,32,128]{2,1,0:T(8,128)(2,1)S(1)}, bf16[32,32,128]{2,1,0:T(8,128)(2,1)S(1)}, u32[]{:S(2)}, u32[]{:S(2)}) collective-permute-start(bf16[32,32,128]{2,1,0:T(8,128)(2,1)S(1)} %copy-done.1), channel_id=1, source_target_pairs={{64,0},{128,64},{192,128},{0,192},{65,1},{129,65},{193,129},{1,193... | collective-permute-start | bytes 786440 | tf_op jit(solution)/shard_map/ppermute | solution.py:481
  123.7 30.1 %collective-permute-start.2 = (bf16[64,2,32,128]{3,2,1,0:T(8,128)(2,1)}, bf16[64,2,32,128]{3,2,1,0:T(8,128)(2,1)S(1)}, u32[]{:S(2)}, u32[]{:S(2)}) collective-permute-start(bf16[64,2,32,128]{3,2,1,0:T(8,128)(2,1)} %all-to-all-done.1), channel_id=1, source_target_pairs={{64,0},{128,64},{192,128},{0,192},{65,1},{129,65},{193,129},{1,193... | collective-permute-start | bytes 3145736 | tf_op jit(solution)/shard_map/ppermute | solution.py:481
  124.6 29.3 %all-to-all-start.2 = ((bf16[64,32,128]{2,1,0:T(8,128)(2,1)}), bf16[64,32,128]{2,1,0:T(8,128)(2,1)S(1)}, u32[]{:S(2)}, u32[]{:S(2)}) async-start(bf16[64,32,128]{2,1,0:T(8,128)(2,1)} %pad_maximum_fusion), calls=%async_computation.2 | async-start | bytes 1048576 | tf_op jit(solution)/shard_map/all_to_all | solution.py:476
